TPU v7x, 128 devices: a whole 4x4x4 slice. The times are simulated.
128 devices in a mesh: dense: 32 (over x, z, core), attn: 4 (over y).
Axes of the slice: x: 4, y: 4, z: 4, core: 2. Of those that a mesh axis runs over, the one named last changes fastest.
Arguments:
- queries: bfloat16 [8192, 4096], P('dense', 'attn'), may hold values from -30 to 30
- keys: bfloat16 [8192, 1024], P('dense', 'attn'), may hold values from -13 to 13
- values: bfloat16 [8192, 1024], P('dense', 'attn'), may hold values from -24 to 24
- segments: int32 [8192], replicated, may hold values from 0 to 5, never falling along the last dimension, each value on 1 to 4096 neighbouring positions
- out_weight: bfloat16 [4096, 4096], P('attn', 'dense'), may hold values from -0.09375 to 0.09375
Outputs:
- projected: bfloat16 [8192, 4096], P('dense', 'attn')
All inputs are finite; a program needn't handle non-finite values.
Results may differ from a plain program's by a relative error of at most 0.012.
Values may be sent and summed in bfloat16 or wider, within the bound.
A program may use at most 128 MiB of HBM per device.

v0:
```python
import math

import jax
import jax.numpy as jnp
from jax import lax
from jax.sharding import PartitionSpec as P

HEAD_WIDTH = 128


NEGATIVE = -1e30


def attend(query_rows, positions, query_docs, keys, values, segments):
    token_count = query_rows.shape[0]
    kv_local = keys.shape[1] // HEAD_WIDTH
    head_group = query_rows.shape[1] // HEAD_WIDTH // kv_local
    blocks_count = max(token_count // 128, 1)
    block_rows = token_count // blocks_count
    inv_root = 1.0 / math.sqrt(HEAD_WIDTH)
    query_heads = query_rows.reshape(token_count, kv_local, head_group, HEAD_WIDTH)
    initial = tuple(
        (
            (
                jnp.full((kv_local, head_group, block_rows), NEGATIVE, jnp.float32),
                jnp.zeros((kv_local, head_group, block_rows), jnp.float32),
                jnp.zeros((kv_local, head_group, block_rows, HEAD_WIDTH), jnp.float32),
            )
            for which_block in range(blocks_count)
        )
    )
    key_piece = lax.all_gather(keys, "dense", axis=0, tiled=True)
    value_piece = lax.all_gather(values, "dense", axis=0, tiled=True)
    key_count = key_piece.shape[0]
    key_positions = jnp.arange(key_count, dtype=jnp.int32)
    key_heads = key_piece.reshape(key_count, kv_local, HEAD_WIDTH)
    value_heads = value_piece.reshape(key_count, kv_local, HEAD_WIDTH)
    updated = []
    for which_block in range(blocks_count):
        lower = which_block * block_rows
        upper = lower + block_rows
        visible = (query_docs[lower:upper, None] == segments[None, :]) & (
            key_positions[None, :] <= positions[lower:upper, None]
        )
        sliced = query_heads[lower:upper]

        def compute(state):
            row_max, totals, summed = state
            scores = (
                jnp.einsum("qgjd,kgd->gjqk", sliced, key_heads, preferred_element_type=jnp.float32)
                * inv_root
            )
            scores = jnp.where(visible, scores, NEGATIVE)
            new_max = jnp.maximum(row_max, jnp.max(scores, axis=-1))
            weights = jnp.where(visible, jnp.exp(scores - new_max[..., None]), 0.0)
            totals = jnp.sum(weights, axis=-1)
            summed = jnp.einsum(
                "gjqk,kgd->gjqd",
                weights.astype(jnp.bfloat16),
                value_heads,
                preferred_element_type=jnp.float32,
            )
            return (new_max, totals, summed)

        updated.append(
            lax.cond(jnp.any(visible), compute, lambda state: state, initial[which_block])
        )
    final = tuple(updated)
    outputs = []
    for state in final:
        outputs.append(state[2] / state[1][..., None])
    attended = jnp.concatenate(outputs, axis=2).astype(jnp.bfloat16)
    return attended.transpose(2, 0, 1, 3).reshape(token_count, kv_local * head_group * HEAD_WIDTH)


def project(attended, out_weight):
    partial_sums = jnp.dot(
        attended,
        lax.all_gather(out_weight, "dense", axis=1, tiled=True),
        preferred_element_type=jnp.float32,
    )
    return lax.psum_scatter(
        partial_sums.astype(jnp.bfloat16), "attn", scatter_dimension=1, tiled=True
    )


def shards(queries, keys, values, segments, out_weight):
    device_index = lax.axis_index("dense")
    token_count = queries.shape[0]
    positions = device_index * token_count + jnp.arange(token_count, dtype=jnp.int32)
    query_docs = lax.dynamic_slice_in_dim(segments, device_index * token_count, token_count)
    attended = attend(queries, positions, query_docs, keys, values, segments)
    projected = project(attended, out_weight)
    return projected


def solution(mesh):
    return jax.shard_map(
        shards,
        mesh=mesh,
        in_specs=(
            P("dense", "attn"),
            P("dense", "attn"),
            P("dense", "attn"),
            P(),
            P("attn", "dense"),
        ),
        out_specs=P("dense", "attn"),
        check_vma=False,
    )
```

profile of v0, /device:TPU:5, one launch (start us, length us, event | category | flops | bytes accessed | tf_op | source)
XLA Modules:
  0.0 250.7 jit_solution(4987157832332547177)
XLA Ops:
  6.5 0.0 all-gather.4.cloned.1.call-start
  6.5 1.7 copy.12
  8.2 0.0 all-gather.4.cloned.1.call-update
  8.2 0.0 all-gather.6.cloned.1.call-start
  8.3 1.6 copy.13
  9.9 0.0 all-gather.6.cloned.1.call-update
  9.9 0.0 all-gather.8.cloned.1.call-start
  10.0 0.7 all-gather.8.cloned.1.call-update
  10.7 0.0 reduce-scatter.2.cloned.1.call-start
  10.7 0.8 dynamic_slice.3
  11.5 4.9 %fusion.27 = (pred[]{:T(512)}, pred[]{:T(512)}, pred[128,8192]{0,1:T(8,128)(4,1)S(1)}, pred[128,8192]{0,1:T(8,128)(4,1)S(1)}) fusion(s32[128]{0:T(128)S(1)} %get-tuple-element.63, s32[8192]{0:T(1024)} %param.12, s32[128]{0:T(128)S(1)} %get-tuple-element.60, s32[128]{0:T(128)S(1)} %get-tuple-element.64, s32[128]{0:T(128)S(1)} %get-tuple-element.59), kind=kLoop, calls=%fused_computation.38 | loop fusion | flops 8388606 | bytes 2131970 | tf_op jit(solution)/shard_map/reduce_or | solution.py:66
  17.6 42.1 %all-gather.4.cloned.1.call-done = bf16[8192,256]{0,1:T(8,128)(2,1)} async-done(((bf16[256,256]{0,1:T(8,128)(2,1)}), bf16[8192,256]{0,1:T(8,128)(2,1)}) %all-gather.4.cloned.1.call-update) | async-done | bytes 4194320 | tf_op jit(solution)/shard_map/all_gather | solution.py:32
  59.7 50.4 %all-gather.6.cloned.1.call-done = bf16[8192,256]{0,1:T(8,128)(2,1)} async-done(((bf16[256,256]{0,1:T(8,128)(2,1)}), bf16[8192,256]{0,1:T(8,128)(2,1)}) %all-gather.6.cloned.1.call-update) | async-done | bytes 4194320 | tf_op jit(solution)/shard_map/all_gather | solution.py:33
  110.0 48.6 %conditional.2 = (f32[2,4,128]{2,1,0:T(4,128)S(1)}, f32[2,4,128,128]{2,3,1,0:T(8,128)S(1)}) conditional(s32[]{:T(128)} %convert_element_type.16, () %tuple.21, (pred[128,8192]{0,1:T(8,128)(4,1)S(1)}, bf16[256,1024]{1,0:T(8,128)(2,1)}, bf16[8192,2,128]{0,2,1:T(8,128)(2,1)}, bf16[8192,2,128]{0,2,1:T(8,128)(2,1)}) %tuple.54), branch_computations={%region_1.0_spmd, %region_2.5_spmd} | conditional | flops 4404018176 | bytes 114581520 | solution.py:66
  110.0 1.2 copy.14
  111.3 16.2 %fusion = (f32[2,4,128]{2,1,0:T(4,128)S(1)}, f32[2,8192,128,4]{2,1,3,0:T(8,128)}) fusion(pred[128,8192]{0,1:T(8,128)(4,1)S(1)} %get-tuple-element.25, bf16[128,2,4,128]{0,3,2,1:T(8,128)(2,1)S(1)} %bitcast.60, bf16[8192,2,128]{0,2,1:T(8,128)(2,1)} %get-tuple-element.43), kind=kOutput, calls=%fused_computation.2 | convolution fusion | flops 2172648448 | bytes 39063552 | tf_op jit(solution)/shard_map/cond/branch_1_fun/qgjd,kgd->gjqk/dot_general | solution.py:50
  127.5 15.5 %fusion.3 = f32[2,4,128,128]{2,3,1,0:T(8,128)S(1)} fusion(f32[2,8192,128,4]{2,1,3,0:T(8,128)} %get-tuple-element.54, f32[2,4,128]{2,1,0:T(4,128)S(1)} %broadcast_maximum_fusion, pred[128,8192]{0,1:T(8,128)(4,1)S(1)} %get-tuple-element.25, bf16[8192,2,128]{0,2,1:T(8,128)(2,1)} %get-tuple-element.44), kind=kOutput, calls=%fused_computation.5 | convolution fusion | flops 2189426688 | bytes 39325696 | tf_op jit(solution)/shard_map/cond | solution.py:66
  143.1 15.5 %fusion.2 = f32[2,4,128]{2,1,0:T(4,128)S(1)} fusion(f32[2,8192,128,4]{2,1,3,0:T(8,128)} %get-tuple-element.54, f32[2,4,128]{2,1,0:T(4,128)S(1)} %broadcast_maximum_fusion, pred[128,8192]{0,1:T(8,128)(4,1)S(1)} %get-tuple-element.25), kind=kLoop, calls=%fused_computation.4 | loop fusion | flops 41942016 | bytes 34611200 | tf_op jit(solution)/shard_map/cond/branch_1_fun/reduce_sum | solution.py:56
  158.6 48.3 %conditional.3 = (f32[2,4,128]{2,1,0:T(4,128)S(1)}, f32[2,4,128,128]{2,3,1,0:T(8,128)S(1)}) conditional(s32[]{:T(128)} %convert_element_type.17, () %tuple.23, (pred[128,8192]{0,1:T(8,128)(4,1)S(1)}, bf16[256,1024]{1,0:T(8,128)(2,1)}, bf16[8192,2,128]{0,2,1:T(8,128)(2,1)}, bf16[8192,2,128]{0,2,1:T(8,128)(2,1)}) %tuple.55), branch_computations={%region_6.7_spmd, %region_7.10_spmd} | conditional | flops 4404018176 | bytes 114581520 | solution.py:66
  158.8 1.2 copy.18
  160.1 16.7 %fusion.12 = (f32[2,4,128]{2,1,0:T(4,128)S(1)}, f32[2,8192,128,4]{2,1,3,0:T(8,128)}) fusion(pred[128,8192]{0,1:T(8,128)(4,1)S(1)} %get-tuple-element.29, bf16[128,2,4,128]{0,3,2,1:T(8,128)(2,1)S(1)} %bitcast.61, bf16[8192,2,128]{0,2,1:T(8,128)(2,1)} %get-tuple-element.47), kind=kOutput, calls=%fused_computation.16 | convolution fusion | flops 2172648448 | bytes 39063552 | tf_op jit(solution)/shard_map/cond/branch_1_fun/qgjd,kgd->gjqk/dot_general | solution.py:50
  176.8 15.4 %fusion.15 = f32[2,4,128,128]{2,3,1,0:T(8,128)S(1)} fusion(f32[2,8192,128,4]{2,1,3,0:T(8,128)} %get-tuple-element.56, f32[2,4,128]{2,1,0:T(4,128)S(1)} %broadcast_maximum_fusion.1, pred[128,8192]{0,1:T(8,128)(4,1)S(1)} %get-tuple-element.29, bf16[8192,2,128]{0,2,1:T(8,128)(2,1)} %get-tuple-element.48), kind=kOutput, calls=%fused_computation.19 | convolution fusion | flops 2189426688 | bytes 39325696 | tf_op jit(solution)/shard_map/cond | solution.py:66
  192.2 14.7 %fusion.14 = f32[2,4,128]{2,1,0:T(4,128)S(1)} fusion(f32[2,8192,128,4]{2,1,3,0:T(8,128)} %get-tuple-element.56, f32[2,4,128]{2,1,0:T(4,128)S(1)} %broadcast_maximum_fusion.1, pred[128,8192]{0,1:T(8,128)(4,1)S(1)} %get-tuple-element.29), kind=kLoop, calls=%fused_computation.18 | loop fusion | flops 41942016 | bytes 34611200 | tf_op jit(solution)/shard_map/cond/branch_1_fun/reduce_sum | solution.py:56
  206.9 0.1 divide_convert_fusion.1
  206.9 0.1 divide_convert_fusion
  207.0 0.1 pad_maximum_fusion
  207.1 0.0 all-gather.8.cloned.1.call-done
  207.1 7.1 %convolution_convert_fusion = bf16[256,4096]{1,0:T(8,128)(2,1)} fusion(bf16[256,1024]{0,1:T(8,128)(2,1)S(1)} %bitcast.59, bf16[1024,4096]{1,0:T(8,128)(2,1)} %all-gather.8.cloned.1.call-done), kind=kOutput, calls=%fused_computation.28 | convolution fusion | flops 2148532224 | bytes 11010048 | tf_op jit(solution)/shard_map/dot_general | solution.py:77
  214.2 0.0 reduce-scatter.2.cloned.1.call-update
  214.2 29.9 %reduce-scatter.2.cloned.1.call-done = bf16[256,1024]{1,0:T(8,128)(2,1)} async-done(((bf16[256,4096]{1,0:T(8,128)(2,1)}), bf16[256,1024]{1,0:T(8,128)(2,1)}) %reduce-scatter.2.cloned.1.call-update) | async-done | bytes 524304 | tf_op jit(solution)/shard_map/reduce_scatter | solution.py:82
  (6 shorter events, 0.1 us)
Async XLA Ops:
  6.5 53.1 %all-gather.4.cloned.1.call-start = ((), (), s32[]{:S(2)}) async-start(), calls=%async_computation.1 | async-start | bytes 4325376 | tf_op jit(solution)/shard_map/all_gather | solution.py:32
  8.2 101.8 %all-gather.6.cloned.1.call-start = ((), (), s32[]{:S(2)}) async-start(), calls=%async_computation.2 | async-start | bytes 4325376 | tf_op jit(solution)/shard_map/all_gather | solution.py:33
  9.9 197.1 %all-gather.8.cloned.1.call-start = ((), (), s32[]{:S(2)}) async-start(), calls=%async_computation.3 | async-start | bytes 8650752 | tf_op jit(solution)/shard_map/all_gather | solution.py:79
  10.7 233.4 %reduce-scatter.2.cloned.1.call-start = ((), (), s32[]{:S(2)}) async-start(), calls=%async_computation.4 | async-start | bytes 2621440 | tf_op jit(solution)/shard_map/reduce_scatter | solution.py:82
Sparse Core Ops, SparseCore 0:
  9.5 50.0 all-gather.3
  61.8 48.1 all-gather.5
  112.2 58.5 all-gather.7
  214.4 29.7 reduce-scatter.1
where the time goes:
time: 252 us; the launch traced here: 251 us
  waiting for transfers between devices  123 us (49%)
  matrix products  71 us (28%)
  other arithmetic  35.3 us (14%)
  between operations  14.3 us (6%)
  local copies, waits for them, and re-layouts  6.61 us (3%)
    all_gather x1, waiting for transfers between devices, attend(): value_piece = lax.all_gather(values, 'dense', axis=0, tiled=True)  50.4 us
    all_gather x1, waiting for transfers between devices, attend(): key_piece = lax.all_gather(keys, 'dense', axis=0, tiled=True)  42.1 us
    dot_general x2, matrix products, compute(): jnp.einsum('qgjd,kgd->gjqk', sliced, key_heads, preferred_element_type=jn...  32.9 us
    cond x2, matrix products, attend(): lax.cond(jnp.any(visible), compute, lambda state: state, initial[which_bl...  30.9 us
    reduce_sum x2, other arithmetic, compute(): totals = jnp.sum(weights, axis=-1)  30.2 us
    reduce_scatter x1, waiting for transfers between devices, project(): lax.psum_scatter(partial_sums.astype(jnp.bfloat16), 'attn', scatter_dimen...  29.9 us
    dot_general x1, matrix products, project(): jnp.dot(attended, lax.all_gather(out_weight, 'dense', axis=1, tiled=True)...  7.11 us
  transfers between devices with their start and end apart: 4, of which 3 were waited for; matrix products, arithmetic and copies ran while one was open for 42% of the time, Pallas kernels for 0%

commit v1 on v0

v1 whole, which is shorter than its diff:
```python
import math

import jax
import jax.numpy as jnp
from jax import lax
from jax.experimental import pallas as pl
from jax.experimental.pallas import tpu as pltpu
from jax.sharding import PartitionSpec as P

MESH = pl.DeviceIdType.MESH
BF = jnp.bfloat16
F32 = jnp.float32
HW = 128
TOK = 512
BIG = 32768.0
SCALE = math.log2(math.e) / math.sqrt(HW)
RT = 256
WA = 320


def kernel(q_hbm, k_hbm, v_hbm, seg_ref, w_hbm, out_hbm,
           qbuf, kvbuf, kabuf, wbuf, m_ref, acc_ref, abuf, psend, precv, pown, fin,
           local_sem, pair_send, pair_recv, kv_recv, w_recv, send_sem, p_send, p_recv, fin_local, fin_send, fin_recv):
    d = lax.axis_index("dense")
    y = lax.axis_index("attn")
    core = lax.rem(d, 2)
    chip = d // 2
    z = lax.rem(chip, 4)
    x = chip // 4
    true = None

    def mod4(n):
        return lax.rem(n + 8, 4)

    def chip_at(dx, dz):
        return mod4(x + dx) * 4 + mod4(z + dz)

    def device_at(dx, dz):
        return (chip_at(dx, dz) * 2 + core, y)

    partner = (chip * 2 + (1 - core), y)

    def when(pred, f):
        if pred is None:
            f()
        else:
            pl.when(pred)(f)

    sends = []

    def both(p, r):
        if p is None:
            return r
        if r is None:
            return p
        return jnp.logical_and(p, r)

    def send(ref_of, recv_sems, dx, dz, ddx, ddz, pred=None, src=None):
        n = len(sends)
        slot = ref_of(chip_at(dx, dz))
        rel = ((dx - ddx) % 4) * 4 + (dz - ddz) % 4

        def make():
            return pltpu.make_async_remote_copy(
                src_ref=slot if src is None else src, dst_ref=slot,
                send_sem=send_sem.at[n], recv_sem=recv_sems(rel),
                device_id=device_at(ddx, ddz), device_id_type=MESH)

        sends.append((pred, make))
        when(pred, lambda: make().start())

    def wait(ref_of, recv_sems, dx, dz, pred=None):
        rel = (dx % 4) * 4 + dz % 4
        slot = ref_of(chip_at(dx, dz))
        when(pred, lambda: pltpu.make_async_remote_copy(
            src_ref=slot, dst_ref=slot, send_sem=send_sem.at[0], recv_sem=recv_sems(rel),
            device_id=partner, device_id_type=MESH).wait_recv())

    def kv_of(j):
        return lambda c: kvbuf.at[c, j]

    def kv_sems(j):
        return lambda rel: kv_recv.at[j, rel]

    def kv_send(j, dx, dz, ddx, ddz, pred=None):
        send(kv_of(j), kv_sems(j), dx, dz, ddx, ddz, pred)

    def kv_wait(j, dx, dz, pred=None):
        wait(kv_of(j), kv_sems(j), dx, dz, pred)

    def w_part(t):
        return (0, WA) if t == 0 else (WA, 1024 - WA)

    def w_of(t):
        lo, n = w_part(t)
        return lambda c: wbuf.at[c, pl.ds(lo, n)]

    def w_sems(t):
        return lambda rel: w_recv.at[t, rel]

    def w_send(t, dx, dz, ddx, ddz, src=None):
        send(w_of(t), w_sems(t), dx, dz, ddx, ddz, None, src)

    def w_wait(t, dx, dz):
        wait(w_of(t), w_sems(t), dx, dz)

    def own_cols(ref, width, which):
        return ref.at[:, pl.ds(pl.multiple_of(which * width, width), width)]

    rows_me = pl.ds(pl.multiple_of(core * 256, 256), 256)
    locals_ = [
        pltpu.make_async_copy(own_cols(k_hbm, HW, core), kvbuf.at[chip, 0, rows_me], local_sem.at[0]),
        pltpu.make_async_copy(own_cols(v_hbm, HW, core), kvbuf.at[chip, 1, rows_me], local_sem.at[1]),
        pltpu.make_async_copy(own_cols(q_hbm, 512, core), qbuf.at[rows_me], local_sem.at[2]),
        pltpu.make_async_copy(w_hbm, wbuf.at[chip], local_sem.at[3]),
    ]
    for c in locals_:
        c.start()

    barrier = pltpu.get_barrier_semaphore()
    peers = [partner, device_at(1, 0), device_at(-1, 0), device_at(0, 1), device_at(0, -1)]
    peers += [(d, mod4(y + n)) for n in (1, 2, 3)]
    for peer in peers:
        pl.semaphore_signal(barrier, inc=1, device_id=peer, device_id_type=MESH)
    pl.semaphore_wait(barrier, len(peers))

    pair = []
    for n, (src, dst) in enumerate((
            (own_cols(k_hbm, HW, 1 - core), kvbuf.at[chip, 0, rows_me]),
            (own_cols(v_hbm, HW, 1 - core), kvbuf.at[chip, 1, rows_me]),
            (own_cols(q_hbm, 512, 1 - core), qbuf.at[rows_me]))):
        pair.append(pltpu.make_async_remote_copy(
            src_ref=src, dst_ref=dst, send_sem=pair_send.at[n], recv_sem=pair_recv.at[n],
            device_id=partner, device_id_type=MESH))
        pair[-1].start()

    for j in (0, 1):
        locals_[j].wait()
        pair[j].wait_recv()
        kv_send(j, 0, 0, 1, 0, x <= 2)
        kv_send(j, 0, 0, 0, 1, z <= 2)
        kv_send(j, 0, 0, 0, -1, z == 0)

    def w_own(t):
        lo, n = w_part(t)
        return w_hbm.at[pl.ds(lo, n)]

    for ddx, ddz in ((0, 1), (0, -1), (-1, 0), (1, 0)):
        for t in (1, 0):
            w_send(t, 0, 0, ddx, ddz, w_own(t))

    def onehot(c):
        row = seg_ref[pl.ds(c, 1), :]
        hot = (lax.broadcasted_iota(jnp.int32, (HW, TOK), 0) == row).astype(F32)
        return hot.T

    own_hot = onehot(chip)
    qa = (own_hot * (-BIG)).astype(BF)

    r1 = x >= 1
    r2 = x >= 2

    def scores(h, half, keys):
        qq = qbuf[half * RT:(half + 1) * RT, h * HW:(h + 1) * HW]
        qc = jnp.concatenate([qq, qa[half * RT:(half + 1) * RT]], axis=1)
        return lax.dot_general(qc, keys, (((1,), (1,)), ((), ())), preferred_element_type=F32)

    def weights(s, mp):
        mc = jnp.max(s, axis=1, keepdims=True)
        mn = jnp.maximum(mp, mc) if mp is not None else jnp.broadcast_to(mc, (RT, HW))
        p = jnp.exp2(s * SCALE - (mn * SCALE)[:, :1])
        return mn, p.astype(BF)

    tiles = [(h, half) for h in range(4) for half in range(2)]

    def own_block():
        keys = jnp.concatenate([kvbuf[chip, 0], (1.0 - own_hot).astype(BF)], axis=1)
        vals = jnp.concatenate([kvbuf[chip, 1], jnp.ones((TOK, HW), BF)], axis=1)

        def masked(h, half):
            n = (half + 1) * RT
            s = scores(h, half, keys[:n])
            r = lax.broadcasted_iota(jnp.int32, (RT, n), 0) + half * RT
            c = lax.broadcasted_iota(jnp.int32, (RT, n), 1)
            return jnp.where(c <= r, s, -2.0 * BIG)

        s = masked(*tiles[0])
        for i, (h, half) in enumerate(tiles):
            nxt = masked(*tiles[i + 1]) if i < 7 else None
            mn, p = weights(s, None)
            rows = slice((h * 2 + half) * RT, (h * 2 + half + 1) * RT)
            m_ref[rows] = mn
            acc_ref[rows] = jnp.dot(p, vals[:(half + 1) * RT], preferred_element_type=F32)
            s = nxt

    def put_mask(c, valid, n):
        hot = onehot(c)
        kabuf[n * TOK:(n + 1) * TOK] = jnp.where(valid, 1.0 - hot, 1.0).astype(BF)

    def two_blocks(ca, cb, part):
        keys = jnp.concatenate([
            jnp.concatenate([kvbuf[ca, 0], kvbuf[cb, 0]], axis=0), kabuf[...]], axis=1)
        vals = jnp.concatenate([
            jnp.concatenate([kvbuf[ca, 1], kvbuf[cb, 1]], axis=0), jnp.ones((2 * TOK, HW), BF)], axis=1)
        todo = tiles[part * 4:part * 4 + 4]
        s = scores(*todo[0], keys)
        for i, (h, half) in enumerate(todo):
            rows = slice((h * 2 + half) * RT, (h * 2 + half + 1) * RT)
            mp = m_ref[rows]
            old = acc_ref[rows]
            nxt = scores(*todo[i + 1], keys) if i < 3 else None
            mn, p = weights(s, mp)
            al = jnp.exp2((mp - mn) * SCALE)
            add = jnp.dot(p, vals, preferred_element_type=F32)
            m_ref[rows] = mn
            acc_ref[rows] = old * jnp.concatenate([al, al], axis=1) + add
            s = nxt

    def kv_x1():
        for j in (0, 1):
            kv_wait(j, -1, 0, r1)
            kv_send(j, -1, 0, 1, 0, both(r1, x <= 2))
            kv_send(j, -1, 0, 0, 1, r1)
            kv_send(j, -1, 0, 0, -1, r1)

    def kv_row0():
        for j in (0, 1):
            kv_wait(j, 0, -1, z >= 1)
            kv_send(j, 0, -1, 0, 1, jnp.logical_or(z == 1, z == 2))

    def kv_x2():
        for j in (0, 1):
            kv_wait(j, -2, 0, r2)
            kv_send(j, -2, 0, 0, -1, both(r2, z >= 1))
            kv_send(j, -2, 0, 0, 1, both(r2, z == 3))

    edge = jnp.logical_or(z == 0, z == 3)
    middle = jnp.logical_or(z == 1, z == 2)

    def kv_row1():
        for j in (0, 1):
            kv_wait(j, -1, -1, r1)
            kv_send(j, -1, -1, 0, 1, both(r1, edge))
            kv_wait(j, -1, 1, r1)
            kv_send(j, -1, 1, 0, -1, both(r1, edge))

    def kv_row2():
        for j in (0, 1):
            kv_wait(j, -2, 1, both(r2, z <= 2))
            kv_send(j, -2, 1, 0, -1, both(r2, middle))

    def kv_last():
        for j in (0, 1):
            kv_wait(j, 0, -2, z >= 2)
            kv_wait(j, 0, 1, z == 3)
            kv_wait(j, -1, 2, r1)
            kv_wait(j, -2, -1, both(r2, z == 0))

    def kv_end():
        for j in (0, 1):
            kv_wait(j, -2, 2, both(r2, z <= 1))

    def place(t, a, b):
        return (a, b) if t == 0 else (b, a)

    def w_first(t, a):
        w_wait(t, *place(t, a, 0))
        if t == 0 and a == -1 or t == 1 and a == 1:
            w_send(t, *place(t, a, 0), *place(t, -a, 0))
        for s in (1, -1):
            w_send(t, *place(t, a, 0), *place(t, 0, s))

    def w_second(t, a, b, relay):
        w_wait(t, *place(t, a, b))
        if relay:
            w_send(t, *place(t, a, b), *place(t, 0, -b))

    def relay2(t, a):
        if t == 1:
            return 1
        return 1 if a in (0, 2) else -1

    def w_far(t):
        w_wait(t, *place(t, 2, 0))
        for s in (1, -1):
            w_send(t, *place(t, 2, 0), *place(t, 0, s))

    def w_line(t, a):
        r = relay2(t, a)
        w_second(t, a, r, True)
        w_second(t, a, -r, False)

    def w_line_far(t, a):
        w_wait(t, *place(t, a, 2))

    locals_[2].wait()
    pair[2].wait_recv()
    own_block()
    kv_x1()
    kv_row0()
    kv_x2()

    def pick(dz):
        zs = mod4(z + dz)
        before = zs < z
        c = jnp.where(before, x * 4, mod4(x - 2) * 4) + zs
        return c, jnp.logical_or(before, r2)

    steps = [
        ((chip_at(-1, 0), r1), (chip_at(-2, 0), r2)),
        ((chip_at(-1, -1), r1), (chip_at(-1, 1), r1)),
        ((chip_at(-1, 2), r1), pick(-1)),
        (pick(1), pick(2)),
    ]
    before = [[], [kv_row1], [kv_row2, kv_last], [kv_end]]
    between = [
        [[lambda: w_first(1, 1), lambda: w_first(1, -1)], [lambda: w_first(0, -1), lambda: w_first(0, 1)]],
        [[lambda: w_line(1, 0)], [lambda: w_far(1)]],
        [[lambda: w_far(0)], [lambda: w_line(0, 0)]],
        [[lambda: w_line(1, 1)], [lambda: w_line(1, -1)]],
    ]

    for s in range(4):
        (ca, va), (cb, vb) = steps[s]
        for f in before[s]:
            f()
        live = jnp.logical_or(va, vb)
        ca = jnp.where(va, ca, chip)
        cb = jnp.where(vb, cb, chip)

        def masks():
            put_mask(ca, va, 0)
            put_mask(cb, vb, 1)

        pl.when(live)(masks)
        for part in (0, 1):
            pl.when(live)(lambda: two_blocks(ca, cb, part))
            for f in between[s][part]:
                f()

    for h in range(4):
        rows = slice(h * TOK, (h + 1) * TOK)
        abuf[core, :, h * HW:(h + 1) * HW] = (acc_ref[rows, :HW] / acc_ref[rows, HW:]).astype(BF)
    swap = pltpu.make_async_remote_copy(
        src_ref=abuf.at[core], dst_ref=abuf.at[core], send_sem=pair_send.at[3], recv_sem=pair_recv.at[3],
        device_id=partner, device_id_type=MESH)
    swap.start()

    for a in (1, -1):
        w_line(0, a)
    w_line(1, 2)
    w_line(0, 2)
    locals_[3].wait()
    swap.wait_recv()

    def quarter(qr, pairs):
        lhs = [abuf[0], abuf[1]]
        for n in pairs:
            wcat = jnp.concatenate([wbuf[qr * 4 + 2 * n], wbuf[qr * 4 + 2 * n + 1]], axis=1)
            part = jnp.dot(lhs[0], wcat[:512], preferred_element_type=F32)
            part += jnp.dot(lhs[1], wcat[512:], preferred_element_type=F32)
            mine = qr == y

            def keep():
                pown[n] = part

            def give():
                slot = mod4(qr - y) - 1
                psend[slot, n] = part.astype(BF)
                p_copy(slot, n).start()

            pl.when(mine)(keep)
            pl.when(jnp.logical_not(mine))(give)

    def p_copy(slot, n):
        return pltpu.make_async_remote_copy(
            src_ref=psend.at[slot, n], dst_ref=precv.at[slot, n],
            send_sem=p_send.at[slot, n], recv_sem=p_recv.at[slot, n],
            device_id=(d, mod4(y + slot + 1)), device_id_type=MESH)

    for a in (0, 1, -1, 2):
        w_line_far(0, a)
    for b in (0, 1, -1, 2):
        w_line_far(1, b)
    for dq in (0, 1, -1, 2):
        quarter(mod4(x + dq), (0, 1))

    for n in (0, 1):
        for slot in range(3):
            p_copy(slot, n).wait_recv()
        total = pown[n]
        for slot in range(3):
            total += precv[slot, n].astype(F32)
        fin[n] = total.astype(BF)
    ends = []
    rows_you = pl.ds(pl.multiple_of((1 - core) * 256, 256), 256)
    for n in range(4):
        cols = pl.ds(pl.multiple_of((2 * n + core) * HW, HW), HW)
        lanes = pl.ds((n % 2) * HW, HW)
        far = pltpu.make_async_remote_copy(
            src_ref=fin.at[n // 2, rows_you, lanes], dst_ref=out_hbm.at[:, cols],
            send_sem=fin_send.at[n], recv_sem=fin_recv.at[n], device_id=partner, device_id_type=MESH)
        far.start()
        near = pltpu.make_async_copy(fin.at[n // 2, rows_me, lanes], out_hbm.at[:, cols], fin_local.at[n])
        near.start()
        ends.append((far, near))
    for far, near in ends:
        far.wait()
        near.wait()
    for c in pair:
        c.wait_send()
    swap.wait_send()
    for pred, make in sends:
        when(pred, lambda: make().wait_send())
    for slot in range(3):
        for n in (0, 1):
            p_copy(slot, n).wait_send()


def shards(queries, keys, values, segments, out_weight):
    return pl.pallas_call(
        kernel,
        out_shape=jax.ShapeDtypeStruct((256, 1024), BF),
        in_specs=[
            pl.BlockSpec(memory_space=pl.ANY),
            pl.BlockSpec(memory_space=pl.ANY),
            pl.BlockSpec(memory_space=pl.ANY),
            pl.BlockSpec(memory_space=pltpu.VMEM),
            pl.BlockSpec(memory_space=pl.ANY),
        ],
        out_specs=pl.BlockSpec(memory_space=pl.ANY),
        scratch_shapes=[
            pltpu.VMEM((TOK, 512), BF),
            pltpu.VMEM((16, 2, TOK, HW), BF),
            pltpu.VMEM((2 * TOK, HW), BF),
            pltpu.VMEM((16, 1024, HW), BF),
            pltpu.VMEM((2048, HW), F32),
            pltpu.VMEM((2048, 2 * HW), F32),
            pltpu.VMEM((2, TOK, 512), BF),
            pltpu.VMEM((3, 2, TOK, 256), BF),
            pltpu.VMEM((3, 2, TOK, 256), BF),
            pltpu.VMEM((2, TOK, 256), F32),
            pltpu.VMEM((2, TOK, 256), BF),
            pltpu.SemaphoreType.DMA((4,)),
            pltpu.SemaphoreType.DMA((4,)),
            pltpu.SemaphoreType.DMA((4,)),
            pltpu.SemaphoreType.DMA((2, 16)),
            pltpu.SemaphoreType.DMA((2, 16)),
            pltpu.SemaphoreType.DMA((80,)),
            pltpu.SemaphoreType.DMA((3, 2)),
            pltpu.SemaphoreType.DMA((3, 2)),
            pltpu.SemaphoreType.DMA((4,)),
            pltpu.SemaphoreType.DMA((4,)),
            pltpu.SemaphoreType.DMA((4,)),
        ],
        compiler_params=pltpu.CompilerParams(
            collective_id=0, has_side_effects=True, vmem_limit_bytes=60 * 2**20),
        name="attention_projection",
    )(queries, keys, values, segments.reshape(16, TOK), out_weight)


def solution(mesh):
    return jax.shard_map(
        shards,
        mesh=mesh,
        in_specs=(
            P("dense", "attn"),
            P("dense", "attn"),
            P("dense", "attn"),
            P(),
            P("attn", "dense"),
        ),
        out_specs=P("dense", "attn"),
        check_vma=False,
    )
```

time: 252 us -> 97.7 us (0.39)
  waiting for transfers between devices: 123 us -> 0 us
  Pallas kernels: 0 us -> 92.7 us
  matrix products: 71 us -> 0 us
  other arithmetic: 35.3 us -> 0 us
  between operations: 14.3 us -> 0.01 us
  local copies, waits for them, and re-layouts: 6.61 us -> 3.25 us
    pallas_call x0 -> x1, Pallas kernels: none -> 92.7 us  [shards(): pl.pallas_call(kernel, out_shape=jax.ShapeDtypeStruct((256, 1024), BF), i...]
    all_gather x3 -> x0, waiting for transfers between devices: 92.4 us -> none  [the longest x1 50.4 us: attend(): value_piece = lax.all_gather(values, 'dense', axis=0, tiled=True)]
    dot_general x3 -> x0, matrix products: 40.1 us -> none  [the longest x2 32.9 us: compute(): jnp.einsum('qgjd,kgd->gjqk', sliced, key_heads, preferred_element_type=jn...]
    cond x2 -> x0, matrix products: 30.9 us -> none  [attend(): lax.cond(jnp.any(visible), compute, lambda state: state, initial[which_bl...]
    reduce_sum x2 -> x0, other arithmetic: 30.2 us -> none  [compute(): totals = jnp.sum(weights, axis=-1)]
    reduce_scatter x1 -> x0, waiting for transfers between devices: 29.9 us -> none  [project(): lax.psum_scatter(partial_sums.astype(jnp.bfloat16), 'attn', scatter_dimen...]
    reduce_or x1 -> x0, other arithmetic: 4.91 us -> none  [attend(): jnp.any(visible)]
  transfers between devices with their start and end apart: 4 -> 0, of which waited for: 3 -> 0; matrix products, arithmetic and copies ran while one was open for 42% -> 0% of each run, Pallas kernels for 0% -> 0%
where the time goes in v1:
time: 97.7 us; the launch traced here: 96 us
  Pallas kernels  92.7 us (95%)
  local copies, waits for them, and re-layouts  3.25 us (3%)
    pallas_call x1, Pallas kernels, shards(): pl.pallas_call(kernel, out_shape=jax.ShapeDtypeStruct((256, 1024), BF), i...  92.7 us

profile of v1, /device:TPU:5, one launch (start us, length us, event | category | flops | bytes accessed | tf_op | source)
XLA Modules:
  0.0 96.0 jit_solution(3360106416446503684)
XLA Ops:
  0.0 1.4 %reshape.3.seg_ref = s32[16,512]{1,0:T(8,128)} reshape(s32[8192]{0:T(1024)} %param.8) | data formatting | bytes 65536 | tf_op jit(solution)/shard_map/reshape | solution.py:459
  1.4 92.7 %attention_projection.1 = bf16[256,1024]{1,0:T(8,128)(2,1)} custom-call(bf16[256,1024]{1,0:T(8,128)(2,1)} %q_hbm.1, bf16[256,256]{1,0:T(8,128)(2,1)} %k_hbm.1, bf16[256,256]{1,0:T(8,128)(2,1)} %v_hbm.1, s32[16,512]{1,0:T(8,128)} %reshape.3.seg_ref, bf16[1024,128]{1,0:T(8,128)(2,1)} %w_hbm.1), custom_call_target="tpu_custom_call" | custom-call | tf_op jit(solution)/shard_map/attention_projection/pallas_call | solution.py:421
  94.1 1.9 %copy.7 = bf16[256,1024]{1,0:T(8,128)(2,1)} copy(bf16[256,1024]{1,0:T(8,128)(2,1)} %attention_projection.1) | data formatting | bytes 1048576

commit v2 on v1

v2 whole, which is shorter than its diff:
```python
import math

import jax
import jax.numpy as jnp
from jax import lax
from jax.experimental import pallas as pl
from jax.experimental.pallas import tpu as pltpu
from jax.sharding import PartitionSpec as P

MESH = pl.DeviceIdType.MESH
BF = jnp.bfloat16
F32 = jnp.float32
HW = 128
TOK = 512
BIG = 32768.0
SCALE = math.log2(math.e) / math.sqrt(HW)
RT = 256


def kernel(q_hbm, k_hbm, v_hbm, seg_ref, w_hbm, out_hbm,
           qbuf, kvbuf, kabuf, wbuf, m_ref, acc_ref, abuf, hold, own, far_out, far_in, near_out, near_in, fin,
           local_sem, pair_send, pair_recv, kv_recv, w_recv, send_sem, a_recv, far_recv, near_recv,
           fin_local, fin_recv):
    d = lax.axis_index("dense")
    y = lax.axis_index("attn")
    core = lax.rem(d, 2)
    chip = d // 2
    z = lax.rem(chip, 4)
    x = chip // 4

    def mod4(n):
        return lax.rem(n + 8, 4)

    def chip_at(dx, dz):
        return mod4(x + dx) * 4 + mod4(z + dz)

    def device_at(dx, dz):
        return (chip_at(dx, dz) * 2 + core, y)

    partner = (chip * 2 + (1 - core), y)
    pair_chip = x * 4 + (z + 1 - 2 * lax.rem(z, 2))
    cross = ((x * 4 + 3 - z) * 2 + core, y)

    def y_at(n):
        return (d, mod4(y + n))

    def when(pred, f):
        if pred is None:
            f()
        else:
            pl.when(pred)(f)

    def both(p, r):
        if p is None:
            return r
        if r is None:
            return p
        return jnp.logical_and(p, r)

    sends = []

    def send(src, dst, recv_sem, device, pred=None):
        n = len(sends)

        def make():
            return pltpu.make_async_remote_copy(
                src_ref=src, dst_ref=dst, send_sem=send_sem.at[n], recv_sem=recv_sem,
                device_id=device, device_id_type=MESH)

        sends.append((pred, make))
        when(pred, lambda: make().start())

    def wait(dst, recv_sem, pred=None):
        when(pred, lambda: pltpu.make_async_remote_copy(
            src_ref=dst, dst_ref=dst, send_sem=send_sem.at[0], recv_sem=recv_sem,
            device_id=partner, device_id_type=MESH).wait_recv())

    def kv_at(c, j, h):
        return kvbuf.at[c, j, pl.ds(pl.multiple_of(h * 256, 256), 256)]

    def kv_send(j, h, dx, dz, ddx, ddz, pred=None):
        slot = kv_at(chip_at(dx, dz), j, h)
        rel = ((dx - ddx) % 4) * 4 + (dz - ddz) % 4
        send(slot, slot, kv_recv.at[j * 2 + h, rel], device_at(ddx, ddz), pred)

    def kv_wait(j, h, dx, dz, pred=None):
        rel = (dx % 4) * 4 + dz % 4
        wait(kv_at(chip_at(dx, dz), j, h), kv_recv.at[j * 2 + h, rel], pred)

    pieces = [(j, h) for j in (0, 1) for h in (0, 1)]

    def w_at(s, row, piece):
        return wbuf.at[s, row, pl.ds(piece * 512, 512)]

    def w_send(s, piece, dx, ddx, src=None):
        slot = w_at(s, mod4(x + dx), piece)
        send(slot if src is None else src, slot, w_recv.at[s * 2 + piece, (dx - ddx) % 4], device_at(ddx, 0))

    def w_wait(s, piece, dx):
        wait(w_at(s, mod4(x + dx), piece), w_recv.at[s * 2 + piece, dx % 4])

    def cols_of(ref, width, which):
        return ref.at[:, pl.ds(pl.multiple_of(which * width, width), width)]

    rows_me = pl.ds(pl.multiple_of(core * 256, 256), 256)
    locals_ = [
        pltpu.make_async_copy(cols_of(k_hbm, HW, core), kv_at(chip, 0, core), local_sem.at[0]),
        pltpu.make_async_copy(cols_of(v_hbm, HW, core), kv_at(chip, 1, core), local_sem.at[1]),
        pltpu.make_async_copy(cols_of(q_hbm, 512, core), qbuf.at[rows_me], local_sem.at[2]),
        pltpu.make_async_copy(w_hbm, wbuf.at[0, x], local_sem.at[3]),
    ]
    for c in locals_:
        c.start()

    barrier = pltpu.get_barrier_semaphore()
    peers = [partner, device_at(1, 0), device_at(-1, 0), device_at(0, 1), device_at(0, -1),
             (pair_chip * 2 + (1 - core), y), y_at(1), y_at(-1)]
    for peer in peers:
        pl.semaphore_signal(barrier, inc=1, device_id=peer, device_id_type=MESH)
    pl.semaphore_wait(barrier, len(peers))

    pair = []
    for n, (src, dst) in enumerate((
            (cols_of(k_hbm, HW, 1 - core), kv_at(chip, 0, core)),
            (cols_of(v_hbm, HW, 1 - core), kv_at(chip, 1, core)),
            (cols_of(q_hbm, 512, 1 - core), qbuf.at[rows_me]))):
        pair.append(pltpu.make_async_remote_copy(
            src_ref=src, dst_ref=dst, send_sem=pair_send.at[n], recv_sem=pair_recv.at[n],
            device_id=partner, device_id_type=MESH))
        pair[-1].start()

    r1 = x >= 1
    r2 = x >= 2
    edge = jnp.logical_or(z == 0, z == 3)
    middle = jnp.logical_or(z == 1, z == 2)

    for mine in (True, False):
        for j in (0, 1):
            h = core if mine else 1 - core
            if mine:
                locals_[j].wait()
            else:
                pair[j].wait_recv()
            kv_send(j, h, 0, 0, 1, 0, x <= 2)
            kv_send(j, h, 0, 0, -1, 0, both(x <= 1, h == 1))
            kv_send(j, h, 0, 0, 0, 1, z <= 2)
            kv_send(j, h, 0, 0, 0, -1, z == 0)

    def w_cross(piece):
        send(w_hbm.at[pl.ds(piece * 512, 512)], w_at(1, x, piece), w_recv.at[2 + piece, 0], cross)

    w_cross(0)

    def onehot(c):
        row = jnp.concatenate([seg_ref[pl.ds(c * 4 + i, 1), :] for i in range(4)], axis=1)
        hot = (lax.broadcasted_iota(jnp.int32, (HW, TOK), 0) == row).astype(F32)
        return hot.T

    own_hot = onehot(chip)
    qa = (own_hot * (-BIG)).astype(BF)

    def scores(h, half, keys):
        qq = qbuf[half * RT:(half + 1) * RT, h * HW:(h + 1) * HW]
        qc = jnp.concatenate([qq, qa[half * RT:(half + 1) * RT]], axis=1)
        return lax.dot_general(qc, keys, (((1,), (1,)), ((), ())), preferred_element_type=F32)

    def weights(s, mp):
        mc = jnp.max(s, axis=1, keepdims=True)
        mn = jnp.maximum(mp, mc) if mp is not None else jnp.broadcast_to(mc, (RT, HW))
        p = jnp.exp2(s * SCALE - (mn * SCALE)[:, :1])
        return mn, p.astype(BF)

    tiles = [(h, half) for half in range(2) for h in range(4)]

    def tile_rows(h, half):
        return slice((h * 2 + half) * RT, (h * 2 + half + 1) * RT)

    def own_block():
        keys = jnp.concatenate([kvbuf[chip, 0], (1.0 - own_hot).astype(BF)], axis=1)
        vals = jnp.concatenate([kvbuf[chip, 1], jnp.ones((TOK, HW), BF)], axis=1)

        def masked(h, half):
            n = (half + 1) * RT
            s = scores(h, half, keys[:n])
            r = lax.broadcasted_iota(jnp.int32, (RT, n), 0) + half * RT
            c = lax.broadcasted_iota(jnp.int32, (RT, n), 1)
            return jnp.where(c <= r, s, -2.0 * BIG)

        s = masked(*tiles[0])
        for i, (h, half) in enumerate(tiles):
            nxt = masked(*tiles[i + 1]) if i < 7 else None
            mn, p = weights(s, None)
            rows = tile_rows(h, half)
            m_ref[rows] = mn
            acc_ref[rows] = jnp.dot(p, vals[:(half + 1) * RT], preferred_element_type=F32)
            s = nxt

    def put_mask(c, valid, n):
        kabuf[n * TOK:(n + 1) * TOK] = jnp.where(valid, 1.0 - onehot(c), 1.0).astype(BF)

    def two_blocks(ca, cb, part):
        keys = jnp.concatenate([
            jnp.concatenate([kvbuf[ca, 0], kvbuf[cb, 0]], axis=0), kabuf[...]], axis=1)
        vals = jnp.concatenate([
            jnp.concatenate([kvbuf[ca, 1], kvbuf[cb, 1]], axis=0), jnp.ones((2 * TOK, HW), BF)], axis=1)
        todo = tiles[part * 4:part * 4 + 4]
        s = scores(*todo[0], keys)
        for i, (h, half) in enumerate(todo):
            rows = tile_rows(h, half)
            mp = m_ref[rows]
            old = acc_ref[rows]
            nxt = scores(*todo[i + 1], keys) if i < 3 else None
            mn, p = weights(s, mp)
            al = jnp.exp2((mp - mn) * SCALE)
            add = jnp.dot(p, vals, preferred_element_type=F32)
            m_ref[rows] = mn
            acc_ref[rows] = old * jnp.concatenate([al, al], axis=1) + add
            s = nxt

    def kv_x1():
        for j, h in pieces:
            kv_wait(j, h, -1, 0, r1)
            if h == 0:
                kv_send(j, h, -1, 0, 1, 0, both(r1, x <= 2))
            kv_send(j, h, -1, 0, 0, 1, r1)
            kv_send(j, h, -1, 0, 0, -1, r1)

    def kv_back():
        outer = jnp.logical_or(x == 0, x == 3)
        for j in (0, 1):
            kv_wait(j, 1, 1, 0, outer)
            kv_send(j, 1, 1, 0, -1, 0, outer)

    def kv_row0():
        for j, h in pieces:
            kv_wait(j, h, 0, -1, z >= 1)
            kv_send(j, h, 0, -1, 0, 1, middle)

    def kv_x2():
        for j, h in pieces:
            kv_wait(j, h, -2, 0, r2)
            kv_send(j, h, -2, 0, 0, -1, both(r2, z >= 1))
            kv_send(j, h, -2, 0, 0, 1, both(r2, z == 3))

    def kv_row1():
        for j, h in pieces:
            kv_wait(j, h, -1, -1, r1)
            kv_send(j, h, -1, -1, 0, 1, both(r1, edge))
            kv_wait(j, h, -1, 1, r1)
            kv_send(j, h, -1, 1, 0, -1, both(r1, edge))

    def kv_row2():
        for j, h in pieces:
            kv_wait(j, h, -2, 1, both(r2, z <= 2))
            kv_send(j, h, -2, 1, 0, -1, both(r2, middle))

    def kv_last():
        for j, h in pieces:
            kv_wait(j, h, 0, -2, z >= 2)
            kv_wait(j, h, 0, 1, z == 3)
            kv_wait(j, h, -1, 2, r1)
            kv_wait(j, h, -2, -1, both(r2, z == 0))

    def kv_end():
        for j, h in pieces:
            kv_wait(j, h, -2, 2, both(r2, z <= 1))

    def w_own():
        for piece in (0, 1):
            for ddx in (-1, 1):
                w_send(0, piece, 0, ddx, w_hbm.at[pl.ds(piece * 512, 512)])

    def w_crossed():
        for piece in (0, 1):
            w_wait(1, piece, 0)
            for ddx in (-1, 1):
                w_send(1, piece, 0, ddx)

    def w_ring(s):
        for piece, a in ((0, -1), (1, 1)):
            w_wait(s, piece, a)
            w_send(s, piece, a, -a)
            w_wait(s, piece, -a)

    def w_far(s):
        for piece in (0, 1):
            w_wait(s, piece, 2)

    locals_[2].wait()
    pair[2].wait_recv()
    own_block()
    kv_x1()
    w_cross(1)
    kv_back()
    w_own()
    kv_row0()
    kv_x2()

    def pick(dz):
        zs = mod4(z + dz)
        before = zs < z
        c = jnp.where(before, x * 4, mod4(x - 2) * 4) + zs
        return c, jnp.logical_or(before, r2)

    steps = [
        ((chip_at(-1, 0), r1), (chip_at(-2, 0), r2)),
        ((chip_at(-1, -1), r1), (chip_at(-1, 1), r1)),
        ((chip_at(-1, 2), r1), pick(-1)),
        (pick(1), pick(2)),
    ]
    before = [[], [kv_row2], [kv_last], [kv_end]]
    between = [
        [[kv_row1], []],
        [[w_crossed], [lambda: w_ring(0)]],
        [[], [lambda: w_ring(1)]],
        [[], []],
    ]

    def a_slot(t, g, hh):
        return abuf.at[t, g, hh * RT:(hh + 1) * RT]

    def attended(hh):
        for h in range(4):
            rows = tile_rows(h, hh)
            abuf[0, core, hh * RT:(hh + 1) * RT, h * HW:(h + 1) * HW] = (
                acc_ref[rows, :HW] / acc_ref[rows, HW:]).astype(BF)
        send(a_slot(0, core, hh), a_slot(1, core, hh), a_recv.at[1, hh], (pair_chip * 2 + core, y))
        send(a_slot(0, core, hh), a_slot(0, core, hh), a_recv.at[0, hh], partner)

    for s in range(4):
        (ca, va), (cb, vb) = steps[s]
        for f in before[s]:
            f()
        live = jnp.logical_or(va, vb)
        ca = jnp.where(va, ca, chip)
        cb = jnp.where(vb, cb, chip)

        def masks():
            put_mask(ca, va, 0)
            put_mask(cb, vb, 1)

        pl.when(live)(masks)
        for part in (0, 1):
            pl.when(live)(lambda: two_blocks(ca, cb, part))
            for f in between[s][part]:
                f()
            if s == 3:
                attended(part)

    def project(t, hh):
        e = 2 * t + hh
        lhs = jnp.concatenate([abuf[t, 0, hh * RT:(hh + 1) * RT], abuf[t, 1, hh * RT:(hh + 1) * RT]], axis=1)

        def part(n):
            q = mod4(y + n)
            return jnp.dot(lhs, jnp.concatenate([wbuf[0, q], wbuf[1, q]], axis=1), preferred_element_type=F32)

        step = 1 if hh == 0 else -1
        far_out[e] = part(2).astype(BF)
        send(far_out.at[e], far_in.at[e], far_recv.at[e], y_at(step))
        back = 1 if step == -1 else 0
        near_out[e, 1 - back] = part(-step).astype(BF)
        send(near_out.at[e, 1 - back], near_in.at[e, 1 - back], near_recv.at[e, 1 - back], y_at(-step))
        hold[e] = part(step)
        own[e] = part(0)

    def forward(t, hh):
        e = 2 * t + hh
        step = 1 if hh == 0 else -1
        slot = 0 if step == 1 else 1
        wait(far_in.at[e], far_recv.at[e])
        near_out[e, slot] = (hold[e] + far_in[e].astype(F32)).astype(BF)
        send(near_out.at[e, slot], near_in.at[e, slot], near_recv.at[e, slot], y_at(step))

    out_cols = [pl.ds(pl.multiple_of((2 * zz + core) * HW, HW), HW) for zz in (z, 3 - z)]

    def finish(t, hh):
        e = 2 * t + hh
        for slot in (0, 1):
            wait(near_in.at[e, slot], near_recv.at[e, slot])
        fin[e] = (own[e] + near_in[e, 0].astype(F32) + near_in[e, 1].astype(F32)).astype(BF)
        for s in (0, 1):
            src = fin.at[e, :, pl.ds(s * HW, HW)]
            dst = out_hbm.at[:, out_cols[s]]
            if t == 1:
                send(src, dst, fin_recv.at[1 + core, s], (pair_chip * 2 + hh, y))
            else:
                pl.when(core == hh)(lambda: pltpu.make_async_copy(src, dst, fin_local.at[s]).start())
                send(src, dst, fin_recv.at[0, s], partner, core != hh)

    w_far(0)
    w_far(1)
    locals_[3].wait()
    for hh in (0, 1):
        wait(a_slot(0, 1 - core, hh), a_recv.at[0, hh])
        project(0, hh)

    def from_pair(hh):
        wait(a_slot(1, core, hh), a_recv.at[1, hh])
        send(a_slot(1, core, hh), a_slot(1, core, hh), a_recv.at[2, hh], partner)

    forward(0, 0)
    from_pair(0)
    forward(0, 1)
    wait(a_slot(1, 1 - core, 0), a_recv.at[2, 0])
    project(1, 0)
    finish(0, 0)
    from_pair(1)
    finish(0, 1)
    wait(a_slot(1, 1 - core, 1), a_recv.at[2, 1])
    project(1, 1)
    forward(1, 0)
    forward(1, 1)
    finish(1, 0)
    finish(1, 1)

    for s in (0, 1):
        for n in range(3):
            wait(out_hbm.at[:, out_cols[s]], fin_recv.at[n, s])
        pltpu.make_async_copy(fin.at[0, :, pl.ds(s * HW, HW)], out_hbm.at[:, out_cols[s]], fin_local.at[s]).wait()
    for c in pair:
        c.wait_send()
    for pred, make in sends:
        when(pred, lambda: make().wait_send())


def shards(queries, keys, values, segments, out_weight):
    anywhere = pl.BlockSpec(memory_space=pl.ANY)
    return pl.pallas_call(
        kernel,
        out_shape=jax.ShapeDtypeStruct((256, 1024), BF),
        in_specs=[anywhere, anywhere, anywhere, pl.BlockSpec(memory_space=pltpu.VMEM), anywhere],
        out_specs=anywhere,
        scratch_shapes=[
            pltpu.VMEM((TOK, 512), BF),
            pltpu.VMEM((16, 2, TOK, HW), BF),
            pltpu.VMEM((2 * TOK, HW), BF),
            pltpu.VMEM((2, 4, 1024, HW), BF),
            pltpu.VMEM((2048, HW), F32),
            pltpu.VMEM((2048, 2 * HW), F32),
            pltpu.VMEM((2, 2, TOK, 512), BF),
            pltpu.VMEM((4, RT, 256), F32),
            pltpu.VMEM((4, RT, 256), F32),
            pltpu.VMEM((4, RT, 256), BF),
            pltpu.VMEM((4, RT, 256), BF),
            pltpu.VMEM((4, 2, RT, 256), BF),
            pltpu.VMEM((4, 2, RT, 256), BF),
            pltpu.VMEM((4, RT, 256), BF),
            pltpu.SemaphoreType.DMA((4,)),
            pltpu.SemaphoreType.DMA((3,)),
            pltpu.SemaphoreType.DMA((3,)),
            pltpu.SemaphoreType.DMA((4, 16)),
            pltpu.SemaphoreType.DMA((4, 4)),
            pltpu.SemaphoreType.DMA((128,)),
            pltpu.SemaphoreType.DMA((3, 2)),
            pltpu.SemaphoreType.DMA((4,)),
            pltpu.SemaphoreType.DMA((4, 2)),
            pltpu.SemaphoreType.DMA((2,)),
            pltpu.SemaphoreType.DMA((3, 2)),
        ],
        compiler_params=pltpu.CompilerParams(
            collective_id=0, has_side_effects=True, vmem_limit_bytes=60 * 2**20),
        name="attention_projection",
    )(queries, keys, values, segments.reshape(64, HW), out_weight)


def solution(mesh):
    return jax.shard_map(
        shards,
        mesh=mesh,
        in_specs=(
            P("dense", "attn"),
            P("dense", "attn"),
            P("dense", "attn"),
            P(),
            P("attn", "dense"),
        ),
        out_specs=P("dense", "attn"),
        check_vma=False,
    )
```

time: 97.7 us -> 75.2 us (0.77)
  the two profiles are of different devices: /device:TPU:5 before, /device:TPU:1 now
where the time goes in v2:
time: 75.2 us; the launch traced here: 75 us
  Pallas kernels  73.1 us (97%)
  local copies, waits for them, and re-layouts  1.87 us (2%)
    pallas_call x1, Pallas kernels, shards(): pl.pallas_call(kernel, out_shape=jax.ShapeDtypeStruct((256, 1024), BF), i...  73.1 us
    unnamed x1, local copies, waits for them, and re-layouts  1.87 us

profile of v2, /device:TPU:1, one launch (start us, length us, event | category | flops | bytes accessed | tf_op | source)
XLA Modules:
  0.0 75.0 jit_solution(11679810767583167451)
XLA Ops:
  0.0 73.1 %attention_projection.1 = bf16[256,1024]{1,0:T(8,128)(2,1)} custom-call(bf16[256,1024]{1,0:T(8,128)(2,1)} %q_hbm.1, bf16[256,256]{1,0:T(8,128)(2,1)} %k_hbm.1, bf16[256,256]{1,0:T(8,128)(2,1)} %v_hbm.1, s32[64,128]{1,0:T(8,128)} %bitcast.1, bf16[1024,128]{1,0:T(8,128)(2,1)} %w_hbm.1), custom_call_target="tpu_custom_call" | custom-call | tf_op jit(solution)/shard_map/attention_projection/pallas_call | solution.py:429
  73.1 1.9 %copy.7 = bf16[256,1024]{1,0:T(8,128)(2,1)} copy(bf16[256,1024]{1,0:T(8,128)(2,1)} %attention_projection.1) | data formatting | bytes 1048576

commit v3 on v2

v3 whole, which is shorter than its diff:
```python
import math

import jax
import jax.numpy as jnp
from jax import lax
from jax.experimental import pallas as pl
from jax.experimental.pallas import tpu as pltpu
from jax.sharding import PartitionSpec as P

MESH = pl.DeviceIdType.MESH
BF = jnp.bfloat16
F32 = jnp.float32
HW = 128
TOK = 512
BIG = 32768.0
SCALE = math.log2(math.e) / math.sqrt(HW)
RT = 256
CHUNKS = ((0, 0, 256), (0, 256, 256), (1, 0, 128), (1, 128, 128), (1, 256, 128), (1, 384, 128))
N = len(CHUNKS)
STEPS = (
    ((-1, 0), (-1, -1)),
    ((-1, 1), (-2, 0)),
    ((-1, 2), (0, -1)),
    ((0, 1), (0, 2)),
)
ORDER = (
    ("ko", 0, 0), ("cr", 0), ("wo", 1, -1), ("ko", 1, 0), ("ko", 0, 1), ("ko", 1, 1), ("X1", 0, 0), ("X1", 0, 1),
    ("X1", 1, 0), ("X1", 1, 1), ("B", 1), ("B", 0), ("wo", 0, 1), ("X2", 0, 0), ("wo", 0, -1), ("wo", 1, 1),
    ("X2", 1, 0), ("X2", 1, 1), ("wr", 0, 1), ("cr", 1), ("wc", 0), ("L3", 0, 0), ("own",), ("Ra", 1, 0),
    ("X2", 0, 1), ("Ra", 0, 0), ("L1", 0, 1), ("Ra", 0, 1), ("R2", 1, 0), ("Rb", 0, 1), ("R0", 0, 0), ("Rb", 1, 0),
    ("R0", 0, 1), ("Rb", 1, 1), ("Rb", 0, 0), ("R2", 0, 0), ("wr", 0, 0), ("R2", 1, 1), ("c", 1, 0), ("c", 1, 1),
    ("R0", 1, 1), ("L3", 1, 1), ("wc", 1), ("R0", 1, 0), ("Ra", 1, 1), ("L3", 1, 0), ("c", 0, 0), ("R2", 0, 1),
    ("L0", 0, 1), ("c", 0, 1), ("L0", 1, 1), ("L0", 0, 0), ("E", 1, 0), ("E", 0, 0), ("L2", 1, 0), ("L1", 1, 0),
    ("L0", 1, 0), ("L2", 0, 1), ("wr", 1, 0), ("L1", 0, 0), ("ww", 0, 0), ("wr", 1, 1), ("E", 1, 1), ("L1", 1, 1),
    ("L2", 1, 1), ("L2", 0, 0), ("L3", 0, 1), ("wf", 0, 1), ("ww", 0, 1), ("c", 2, 0), ("E", 0, 1), ("c", 3, 0),
    ("at", 0), ("c", 2, 1), ("ww", 1, 1), ("ww", 1, 0), ("wf", 0, 0), ("h", 0), ("c", 3, 1), ("wf", 1, 1),
    ("wf", 1, 0), ("p", 0), ("at", 1), ("h", 1), ("p", 1), ("g", 2), ("g", 3), ("h", 2), ("p", 2), ("h", 3),
    ("g", 4), ("p", 3), ("f", 1), ("h", 4), ("p", 4), ("f", 2), ("g", 5), ("f", 4), ("h", 5), ("p", 5), ("f", 3),
    ("x", 2), ("x", 4), ("f", 0), ("f", 5), ("x", 3), ("x", 5), ("x", 1), ("x", 0),
)

def kernel(q_hbm, k_hbm, v_hbm, seg_ref, w_hbm, out_hbm,
           qbuf, kvbuf, kabuf, wbuf, m_ref, acc_ref, abuf, hold, own, far_out, far_in, near_out, near_in, fin,
           local_sem, pair_send, pair_recv, kv_recv, w_recv, send_sem, a_recv, far_recv, near_recv,
           fin_local, fin_recv):
    d = lax.axis_index("dense")
    y = lax.axis_index("attn")
    core = lax.rem(d, 2)
    chip = d // 2
    z = lax.rem(chip, 4)
    x = chip // 4

    def mod4(n):
        return lax.rem(n + 8, 4)

    def chip_at(dx, dz):
        return mod4(x + dx) * 4 + mod4(z + dz)

    def device_at(dx, dz):
        return (chip_at(dx, dz) * 2 + core, y)

    partner = (chip * 2 + (1 - core), y)
    pair_chip = x * 4 + (z + 1 - 2 * lax.rem(z, 2))
    cross = ((x * 4 + 3 - z) * 2 + core, y)

    def y_at(n):
        return (d, mod4(y + n))

    def when(pred, f):
        if pred is None:
            f()
        else:
            pl.when(pred)(f)

    def both(p, r):
        if p is None:
            return r
        if r is None:
            return p
        return jnp.logical_and(p, r)

    sends = []

    def send(src, dst, recv_sem, device, pred=None):
        n = len(sends)

        def make():
            return pltpu.make_async_remote_copy(
                src_ref=src, dst_ref=dst, send_sem=send_sem.at[n], recv_sem=recv_sem,
                device_id=device, device_id_type=MESH)

        sends.append((pred, make))
        when(pred, lambda: make().start())

    def wait(dst, recv_sem, pred=None):
        when(pred, lambda: pltpu.make_async_remote_copy(
            src_ref=dst, dst_ref=dst, send_sem=send_sem.at[0], recv_sem=recv_sem,
            device_id=partner, device_id_type=MESH).wait_recv())

    def kv_at(c, j, h):
        return kvbuf.at[c, j, pl.ds(pl.multiple_of(h * 256, 256), 256)]

    def kv_send(j, h, dx, dz, ddx, ddz, pred=None):
        slot = kv_at(chip_at(dx, dz), j, h)
        rel = ((dx - ddx) % 4) * 4 + (dz - ddz) % 4
        send(slot, slot, kv_recv.at[j * 2 + h, rel], device_at(ddx, ddz), pred)

    def kv_wait(j, h, dx, dz, pred=None):
        rel = (dx % 4) * 4 + dz % 4
        wait(kv_at(chip_at(dx, dz), j, h), kv_recv.at[j * 2 + h, rel], pred)

    pieces = [(j, h) for j in (0, 1) for h in (0, 1)]

    def w_at(s, row, piece):
        return wbuf.at[s, row, pl.ds(piece * 512, 512)]

    def w_send(s, piece, dx, ddx, src=None):
        slot = w_at(s, mod4(x + dx), piece)
        send(slot if src is None else src, slot, w_recv.at[s * 2 + piece, (dx - ddx) % 4], device_at(ddx, 0))

    def w_wait(s, piece, dx):
        wait(w_at(s, mod4(x + dx), piece), w_recv.at[s * 2 + piece, dx % 4])

    def cols_of(ref, width, which):
        return ref.at[:, pl.ds(pl.multiple_of(which * width, width), width)]

    rows_me = pl.ds(pl.multiple_of(core * 256, 256), 256)
    locals_ = [
        pltpu.make_async_copy(cols_of(k_hbm, HW, core), kv_at(chip, 0, core), local_sem.at[0]),
        pltpu.make_async_copy(cols_of(v_hbm, HW, core), kv_at(chip, 1, core), local_sem.at[1]),
        pltpu.make_async_copy(cols_of(q_hbm, 512, core), qbuf.at[rows_me], local_sem.at[2]),
        pltpu.make_async_copy(w_hbm, wbuf.at[0, x], local_sem.at[3]),
    ]
    for c in locals_:
        c.start()

    barrier = pltpu.get_barrier_semaphore()
    peers = [partner, device_at(1, 0), device_at(-1, 0), device_at(0, 1), device_at(0, -1),
             (pair_chip * 2 + (1 - core), y), y_at(1), y_at(-1)]
    for peer in peers:
        pl.semaphore_signal(barrier, inc=1, device_id=peer, device_id_type=MESH)
    pl.semaphore_wait(barrier, len(peers))

    pair = []
    for n, (src, dst) in enumerate((
            (cols_of(k_hbm, HW, 1 - core), kv_at(chip, 0, core)),
            (cols_of(v_hbm, HW, 1 - core), kv_at(chip, 1, core)),
            (cols_of(q_hbm, 512, 1 - core), qbuf.at[rows_me]))):
        pair.append(pltpu.make_async_remote_copy(
            src_ref=src, dst_ref=dst, send_sem=pair_send.at[n], recv_sem=pair_recv.at[n],
            device_id=partner, device_id_type=MESH))
        pair[-1].start()

    r1 = x >= 1
    r2 = x >= 2
    edge = jnp.logical_or(z == 0, z == 3)
    middle = jnp.logical_or(z == 1, z == 2)

    def kv_own(theirs, j):
        h = 1 - core if theirs else core
        if theirs:
            pair[j].wait_recv()
        else:
            locals_[j].wait()
        kv_send(j, h, 0, 0, 1, 0, x <= 2)
        kv_send(j, h, 0, 0, -1, 0, both(x <= 1, h == 1))
        kv_send(j, h, 0, 0, 0, 1, z <= 2)
        kv_send(j, h, 0, 0, 0, -1, z == 0)

    def w_cross(piece):
        send(w_hbm.at[pl.ds(piece * 512, 512)], w_at(1, x, piece), w_recv.at[2 + piece, 0], cross)

    def onehot(c):
        row = jnp.concatenate([seg_ref[pl.ds(c * 4 + i, 1), :] for i in range(4)], axis=1)
        hot = (lax.broadcasted_iota(jnp.int32, (HW, TOK), 0) == row).astype(F32)
        return hot.T

    own_hot = onehot(chip)
    qa = (own_hot * (-BIG)).astype(BF)

    def scores(h, half, keys):
        qq = qbuf[half * RT:(half + 1) * RT, h * HW:(h + 1) * HW]
        qc = jnp.concatenate([qq, qa[half * RT:(half + 1) * RT]], axis=1)
        return lax.dot_general(qc, keys, (((1,), (1,)), ((), ())), preferred_element_type=F32)

    def weights(s, mp):
        mc = jnp.max(s, axis=1, keepdims=True)
        mn = jnp.maximum(mp, mc) if mp is not None else jnp.broadcast_to(mc, (RT, HW))
        p = jnp.exp2(s * SCALE - (mn * SCALE)[:, :1])
        return mn, p.astype(BF)

    tiles = [(h, half) for half in range(2) for h in range(4)]

    def tile_rows(h, half):
        return slice((h * 2 + half) * RT, (h * 2 + half + 1) * RT)

    def own_block():
        keys = jnp.concatenate([kvbuf[chip, 0], (1.0 - own_hot).astype(BF)], axis=1)
        vals = jnp.concatenate([kvbuf[chip, 1], jnp.ones((TOK, HW), BF)], axis=1)

        def masked(h, half):
            n = (half + 1) * RT
            s = scores(h, half, keys[:n])
            r = lax.broadcasted_iota(jnp.int32, (RT, n), 0) + half * RT
            c = lax.broadcasted_iota(jnp.int32, (RT, n), 1)
            return jnp.where(c <= r, s, -2.0 * BIG)

        s = masked(*tiles[0])
        for i, (h, half) in enumerate(tiles):
            nxt = masked(*tiles[i + 1]) if i < 7 else None
            mn, p = weights(s, None)
            rows = tile_rows(h, half)
            m_ref[rows] = mn
            acc_ref[rows] = jnp.dot(p, vals[:(half + 1) * RT], preferred_element_type=F32)
            s = nxt

    def put_mask(si, c, valid, n):
        kabuf[si, n * TOK:(n + 1) * TOK] = jnp.where(valid, 1.0 - onehot(c), 1.0).astype(BF)

    def two_blocks(si, ca, cb, part):
        keys = jnp.concatenate([
            jnp.concatenate([kvbuf[ca, 0], kvbuf[cb, 0]], axis=0), kabuf[si]], axis=1)
        vals = jnp.concatenate([
            jnp.concatenate([kvbuf[ca, 1], kvbuf[cb, 1]], axis=0), jnp.ones((2 * TOK, HW), BF)], axis=1)
        todo = tiles[part * 4:part * 4 + 4]
        s = scores(*todo[0], keys)
        for i, (h, half) in enumerate(todo):
            rows = tile_rows(h, half)
            mp = m_ref[rows]
            old = acc_ref[rows]
            nxt = scores(*todo[i + 1], keys) if i < 3 else None
            mn, p = weights(s, mp)
            al = jnp.exp2((mp - mn) * SCALE)
            add = jnp.dot(p, vals, preferred_element_type=F32)
            m_ref[rows] = mn
            acc_ref[rows] = old * jnp.concatenate([al, al], axis=1) + add
            s = nxt

    outer = jnp.logical_or(x == 0, x == 3)

    def kv_x1(j, h):
        kv_wait(j, h, -1, 0, r1)
        if h == 0:
            kv_send(j, h, -1, 0, 1, 0, both(r1, x <= 2))
        kv_send(j, h, -1, 0, 0, 1, r1)
        kv_send(j, h, -1, 0, 0, -1, r1)

    def kv_back(j):
        kv_wait(j, 1, 1, 0, outer)
        kv_send(j, 1, 1, 0, -1, 0, outer)

    def kv_row0(j, h):
        kv_wait(j, h, 0, -1, z >= 1)
        kv_send(j, h, 0, -1, 0, 1, middle)

    def kv_x2(j, h):
        kv_wait(j, h, -2, 0, r2)
        kv_send(j, h, -2, 0, 0, -1, both(r2, z >= 1))
        kv_send(j, h, -2, 0, 0, 1, both(r2, z == 3))

    def kv_row1(a):
        def f(j, h):
            kv_wait(j, h, -1, a, r1)
            kv_send(j, h, -1, a, 0, -a, both(r1, edge))
        return f

    def kv_row2(j, h):
        kv_wait(j, h, -2, 1, both(r2, z <= 2))
        kv_send(j, h, -2, 1, 0, -1, both(r2, middle))

    def w_own(piece, ddx):
        w_send(0, piece, 0, ddx, w_hbm.at[pl.ds(piece * 512, 512)])

    def w_crossed(piece):
        w_wait(1, piece, 0)
        for ddx in (-1, 1):
            w_send(1, piece, 0, ddx)

    def w_ring(s, piece):
        a = 2 * piece - 1
        w_wait(s, piece, a)
        w_send(s, piece, a, -a)

    def pick(dz):
        zs = mod4(z + dz)
        before = zs < z
        c = jnp.where(before, x * 4, mod4(x - 2) * 4) + zs
        return c, jnp.logical_or(before, r2)

    def block(b):
        if b[0] == 0:
            return pick(b[1])
        return chip_at(*b), (r1 if b[0] == -1 else r2)

    def step(si, part):
        (ca, va), (cb, vb) = [block(b) for b in STEPS[si]]
        ca = jnp.where(va, ca, chip)
        cb = jnp.where(vb, cb, chip)

        def run():
            if part == 0:
                put_mask(si, ca, va, 0)
                put_mask(si, cb, vb, 1)
            two_blocks(si, ca, cb, part)

        pl.when(jnp.logical_or(va, vb))(run)

    def own_step():
        locals_[2].wait()
        pair[2].wait_recv()
        own_block()

    def a_slot(t, g, lo, n):
        return abuf.at[t, g, lo:lo + n]

    def attended(hh):
        for h in range(4):
            rows = tile_rows(h, hh)
            abuf[0, core, hh * RT:(hh + 1) * RT, h * HW:(h + 1) * HW] = (
                acc_ref[rows, :HW] / acc_ref[rows, HW:]).astype(BF)
        for e, (t, lo, n) in enumerate(CHUNKS):
            if lo // RT == hh:
                to = a_slot(t, core, lo, n)
                send(a_slot(0, core, lo, n), to, a_recv.at[e, 0],
                     (pair_chip * 2 + core, y) if t == 1 else partner)

    def way(e):
        return 1 if e % 2 == 0 else -1

    def near(e, up):
        n = CHUNKS[e][2]
        slot = 0 if up == 1 else 1
        return (near_out.at[e, slot, :n], near_in.at[e, slot, :n], near_recv.at[e, slot])

    def project(e):
        t, lo, n = CHUNKS[e]
        lhs = jnp.concatenate([abuf[t, 0, lo:lo + n], abuf[t, 1, lo:lo + n]], axis=1)

        def part(k):
            q = mod4(y + k)
            return jnp.dot(lhs, jnp.concatenate([wbuf[0, q], wbuf[1, q]], axis=1), preferred_element_type=F32)

        step = way(e)
        far_out[e, :n] = part(2).astype(BF)
        send(far_out.at[e, :n], far_in.at[e, :n], far_recv.at[e], y_at(step))
        src, dst, sem = near(e, -step)
        src[...] = part(-step).astype(BF)
        send(src, dst, sem, y_at(-step))
        hold[e, :n] = part(step)
        own[e, :n] = part(0)

    def forward(e):
        n = CHUNKS[e][2]
        step = way(e)
        wait(far_in.at[e, :n], far_recv.at[e])
        src, dst, sem = near(e, step)
        src[...] = (hold[e, :n] + far_in[e, :n].astype(F32)).astype(BF)
        send(src, dst, sem, y_at(step))

    out_cols = [pl.ds(pl.multiple_of((2 * zz + core) * HW, HW), HW) for zz in (z, 3 - z)]

    def finish(e):
        t, lo, n = CHUNKS[e]
        hh = lo // RT
        for up in (1, -1):
            _, dst, sem = near(e, up)
            wait(dst, sem)
        fin[e, :n] = (own[e, :n] + near_in[e, 0, :n].astype(F32) + near_in[e, 1, :n].astype(F32)).astype(BF)
        for s in (0, 1):
            src = fin.at[e, :n, pl.ds(s * HW, HW)]
            dst = out_hbm.at[pl.ds(lo - hh * RT, n), out_cols[s]]
            if t == 1:
                send(src, dst, fin_recv.at[e, core, s], (pair_chip * 2 + hh, y))
            else:
                pl.when(core == hh)(lambda: pltpu.make_async_copy(src, dst, fin_local.at[s]).start())
                send(src, dst, fin_recv.at[e, 0, s], partner, core != hh)

    def from_pair(e):
        _, lo, n = CHUNKS[e]
        wait(a_slot(1, core, lo, n), a_recv.at[e, 0])
        send(a_slot(1, core, lo, n), a_slot(1, core, lo, n), a_recv.at[e, 1], partner)

    def have(e):
        t, lo, n = CHUNKS[e]
        wait(a_slot(t, 1 - core, lo, n), a_recv.at[e, t])

    actions = {
        "ko": kv_own, "cr": w_cross, "own": own_step, "X1": kv_x1, "B": kv_back, "R0": kv_row0, "X2": kv_x2,
        "Ra": kv_row1(-1), "Rb": kv_row1(1), "R2": kv_row2,
        "L0": lambda j, h: kv_wait(j, h, 0, -2, z >= 2),
        "L1": lambda j, h: kv_wait(j, h, 0, 1, z == 3),
        "L2": lambda j, h: kv_wait(j, h, -1, 2, r1),
        "L3": lambda j, h: kv_wait(j, h, -2, -1, both(r2, z == 0)),
        "E": lambda j, h: kv_wait(j, h, -2, 2, both(r2, z <= 1)),
        "wo": w_own, "wc": w_crossed, "wr": w_ring,
        "ww": lambda s, piece: w_wait(s, piece, 1 - 2 * piece),
        "wf": lambda s, piece: w_wait(s, piece, 2),
        "c": step, "at": attended,
        "h": have, "p": project, "f": forward, "g": from_pair, "x": finish,
    }
    started = False
    for name, *args in ORDER:
        if name == "p" and not started:
            started = True
            locals_[3].wait()
        actions[name](*args)

    for s in (0, 1):
        for e, (t, lo, n) in enumerate(CHUNKS):
            hh = lo // RT
            dst = out_hbm.at[pl.ds(lo - hh * RT, n), out_cols[s]]
            if t == 1:
                for c in (0, 1):
                    wait(dst, fin_recv.at[e, c, s], core == hh)
            else:
                wait(dst, fin_recv.at[e, 0, s], core == hh)
        pltpu.make_async_copy(fin.at[0, :, pl.ds(s * HW, HW)], out_hbm.at[:, out_cols[s]], fin_local.at[s]).wait()
    for c in pair:
        c.wait_send()
    for pred, make in sends:
        when(pred, lambda: make().wait_send())


def shards(queries, keys, values, segments, out_weight):
    anywhere = pl.BlockSpec(memory_space=pl.ANY)
    return pl.pallas_call(
        kernel,
        out_shape=jax.ShapeDtypeStruct((256, 1024), BF),
        in_specs=[anywhere, anywhere, anywhere, pl.BlockSpec(memory_space=pltpu.VMEM), anywhere],
        out_specs=anywhere,
        scratch_shapes=[
            pltpu.VMEM((TOK, 512), BF),
            pltpu.VMEM((16, 2, TOK, HW), BF),
            pltpu.VMEM((4, 2 * TOK, HW), BF),
            pltpu.VMEM((2, 4, 1024, HW), BF),
            pltpu.VMEM((2048, HW), F32),
            pltpu.VMEM((2048, 2 * HW), F32),
            pltpu.VMEM((2, 2, TOK, 512), BF),
            pltpu.VMEM((N, RT, 256), F32),
            pltpu.VMEM((N, RT, 256), F32),
            pltpu.VMEM((N, RT, 256), BF),
            pltpu.VMEM((N, RT, 256), BF),
            pltpu.VMEM((N, 2, RT, 256), BF),
            pltpu.VMEM((N, 2, RT, 256), BF),
            pltpu.VMEM((N, RT, 256), BF),
            pltpu.SemaphoreType.DMA((4,)),
            pltpu.SemaphoreType.DMA((3,)),
            pltpu.SemaphoreType.DMA((3,)),
            pltpu.SemaphoreType.DMA((4, 16)),
            pltpu.SemaphoreType.DMA((4, 4)),
            pltpu.SemaphoreType.DMA((160,)),
            pltpu.SemaphoreType.DMA((N, 2)),
            pltpu.SemaphoreType.DMA((N,)),
            pltpu.SemaphoreType.DMA((N, 2)),
            pltpu.SemaphoreType.DMA((2,)),
            pltpu.SemaphoreType.DMA((N, 2, 2)),
        ],
        compiler_params=pltpu.CompilerParams(
            collective_id=0, has_side_effects=True, vmem_limit_bytes=60 * 2**20),
        name="attention_projection",
    )(queries, keys, values, segments.reshape(64, HW), out_weight)


def solution(mesh):
    return jax.shard_map(
        shards,
        mesh=mesh,
        in_specs=(
            P("dense", "attn"),
            P("dense", "attn"),
            P("dense", "attn"),
            P(),
            P("attn", "dense"),
        ),
        out_specs=P("dense", "attn"),
        check_vma=False,
    )
```

time: 75.2 us -> 67.8 us (0.902)
  the two profiles are of different devices: /device:TPU:1 before, /device:TPU:5 now
where the time goes in v3:
time: 67.8 us; the launch traced here: 67 us
  Pallas kernels  65.1 us (96%)
  local copies, waits for them, and re-layouts  1.87 us (3%)
    pallas_call x1, Pallas kernels, shards(): pl.pallas_call(kernel, out_shape=jax.ShapeDtypeStruct((256, 1024), BF), i...  65.1 us
    unnamed x1, local copies, waits for them, and re-layouts  1.87 us

profile of v3, /device:TPU:5, one launch (start us, length us, event | category | flops | bytes accessed | tf_op | source)
XLA Modules:
  0.0 67.0 jit_solution(1665065411170393852)
XLA Ops:
  0.0 65.1 %attention_projection.1 = bf16[256,1024]{1,0:T(8,128)(2,1)} custom-call(bf16[256,1024]{1,0:T(8,128)(2,1)} %q_hbm.1, bf16[256,256]{1,0:T(8,128)(2,1)} %k_hbm.1, bf16[256,256]{1,0:T(8,128)(2,1)} %v_hbm.1, s32[64,128]{1,0:T(8,128)} %bitcast.1, bf16[1024,128]{1,0:T(8,128)(2,1)} %w_hbm.1), custom_call_target="tpu_custom_call" | custom-call | tf_op jit(solution)/shard_map/attention_projection/pallas_call | solution.py:426
  65.1 1.9 %copy.7 = bf16[256,1024]{1,0:T(8,128)(2,1)} copy(bf16[256,1024]{1,0:T(8,128)(2,1)} %attention_projection.1) | data formatting | bytes 1048576

commit v4 on v3

--- a/solution.py
+++ b/solution.py
@@ -15,28 +15,32 @@
 BIG = 32768.0
 SCALE = math.log2(math.e) / math.sqrt(HW)
 RT = 256
-CHUNKS = ((0, 0, 256), (0, 256, 256), (1, 0, 128), (1, 128, 128), (1, 256, 128), (1, 384, 128))
+CHUNKS = ((0, 0, 256, 2), (0, 256, 256, 2), (1, 0, 128, 2), (1, 128, 128, 2), (1, 256, 128, 2), (1, 384, 128, 2))
 N = len(CHUNKS)
 STEPS = (
-    ((-1, 0), (-1, -1)),
-    ((-1, 1), (-2, 0)),
-    ((-1, 2), (0, -1)),
-    ((0, 1), (0, 2)),
+    ((-1, 0),),
+    ((-1, -1), (-1, 1)),
+    ((-2, 0),),
+    ((-1, 2),),
+    ((0, -1),),
+    ((0, 1),),
+    ((0, 2),),
 )
 ORDER = (
-    ("ko", 0, 0), ("cr", 0), ("wo", 1, -1), ("ko", 1, 0), ("ko", 0, 1), ("ko", 1, 1), ("X1", 0, 0), ("X1", 0, 1),
-    ("X1", 1, 0), ("X1", 1, 1), ("B", 1), ("B", 0), ("wo", 0, 1), ("X2", 0, 0), ("wo", 0, -1), ("wo", 1, 1),
-    ("X2", 1, 0), ("X2", 1, 1), ("wr", 0, 1), ("cr", 1), ("wc", 0), ("L3", 0, 0), ("own",), ("Ra", 1, 0),
-    ("X2", 0, 1), ("Ra", 0, 0), ("L1", 0, 1), ("Ra", 0, 1), ("R2", 1, 0), ("Rb", 0, 1), ("R0", 0, 0), ("Rb", 1, 0),
-    ("R0", 0, 1), ("Rb", 1, 1), ("Rb", 0, 0), ("R2", 0, 0), ("wr", 0, 0), ("R2", 1, 1), ("c", 1, 0), ("c", 1, 1),
-    ("R0", 1, 1), ("L3", 1, 1), ("wc", 1), ("R0", 1, 0), ("Ra", 1, 1), ("L3", 1, 0), ("c", 0, 0), ("R2", 0, 1),
-    ("L0", 0, 1), ("c", 0, 1), ("L0", 1, 1), ("L0", 0, 0), ("E", 1, 0), ("E", 0, 0), ("L2", 1, 0), ("L1", 1, 0),
-    ("L0", 1, 0), ("L2", 0, 1), ("wr", 1, 0), ("L1", 0, 0), ("ww", 0, 0), ("wr", 1, 1), ("E", 1, 1), ("L1", 1, 1),
-    ("L2", 1, 1), ("L2", 0, 0), ("L3", 0, 1), ("wf", 0, 1), ("ww", 0, 1), ("c", 2, 0), ("E", 0, 1), ("c", 3, 0),
-    ("at", 0), ("c", 2, 1), ("ww", 1, 1), ("ww", 1, 0), ("wf", 0, 0), ("h", 0), ("c", 3, 1), ("wf", 1, 1),
-    ("wf", 1, 0), ("p", 0), ("at", 1), ("h", 1), ("p", 1), ("g", 2), ("g", 3), ("h", 2), ("p", 2), ("h", 3),
-    ("g", 4), ("p", 3), ("f", 1), ("h", 4), ("p", 4), ("f", 2), ("g", 5), ("f", 4), ("h", 5), ("p", 5), ("f", 3),
-    ("x", 2), ("x", 4), ("f", 0), ("f", 5), ("x", 3), ("x", 5), ("x", 1), ("x", 0),
+    ("cr", 0), ("cr", 1), ("ko", 0, 0), ("ko", 0, 1), ("ko", 1, 1), ("ko", 1, 0), ("wo", 1, -1), ("X1", 0, 0),
+    ("X1", 1, 0), ("wo", 0, 1), ("B", 0), ("B", 1), ("X1", 1, 1), ("wc", 0), ("own",), ("X2", 0, 0), ("X1", 0, 1),
+    ("wc", 1), ("X2", 1, 1), ("wo", 0, -1), ("X2", 1, 0), ("X2", 0, 1), ("wr", 0, 0), ("c", 0, 0), ("L1", 1, 1),
+    ("R2", 0, 0), ("wo", 1, 1), ("Ra", 0, 0), ("c", 2, 0), ("L1", 0, 1), ("R0", 0, 0), ("c", 0, 1), ("Ra", 1, 0),
+    ("R2", 1, 1), ("R0", 1, 1), ("L1", 0, 0), ("wr", 0, 1), ("c", 2, 1), ("R2", 1, 0), ("Rb", 0, 0), ("R0", 0, 1),
+    ("wr", 1, 0), ("ww", 1, 0), ("R0", 1, 0), ("wr", 1, 1), ("Ra", 1, 1), ("L1", 1, 0), ("L3", 1, 1), ("L3", 0, 0),
+    ("L3", 1, 0), ("R2", 0, 1), ("c", 5, 0), ("L3", 0, 1), ("Ra", 0, 1), ("Rb", 1, 0), ("Rb", 1, 1), ("Rb", 0, 1),
+    ("c", 1, 0), ("ww", 1, 1), ("c", 4, 0), ("L0", 0, 0), ("L2", 0, 0), ("c", 1, 1), ("E", 0, 0), ("E", 0, 1),
+    ("L0", 1, 0), ("L0", 0, 1), ("E", 1, 0), ("E", 1, 1), ("L2", 1, 0), ("L0", 1, 1), ("c", 6, 0), ("L2", 1, 1),
+    ("L2", 0, 1), ("c", 3, 0), ("at", 0), ("ww", 0, 1), ("c", 4, 1), ("c", 6, 1), ("wf", 0, 0), ("wf", 1, 0),
+    ("wf", 0, 1), ("wf", 1, 1), ("h", 0), ("c", 5, 1), ("ww", 0, 0), ("p", 0), ("c", 3, 1), ("g", 2), ("at", 1),
+    ("h", 2), ("p", 2), ("g", 3), ("h", 1), ("p", 1), ("h", 3), ("g", 4), ("p", 3), ("f", 2), ("h", 4), ("p", 4),
+    ("g", 5), ("h", 5), ("p", 5), ("f", 3), ("x", 2), ("f", 4), ("f", 5), ("f", 1), ("f", 0), ("x", 3), ("x", 4),
+    ("x", 5), ("x", 0), ("x", 1),
 )
 
 def kernel(q_hbm, k_hbm, v_hbm, seg_ref, w_hbm, out_hbm,
@@ -217,11 +221,17 @@
     def put_mask(si, c, valid, n):
         kabuf[si, n * TOK:(n + 1) * TOK] = jnp.where(valid, 1.0 - onehot(c), 1.0).astype(BF)
 
-    def two_blocks(si, ca, cb, part):
-        keys = jnp.concatenate([
-            jnp.concatenate([kvbuf[ca, 0], kvbuf[cb, 0]], axis=0), kabuf[si]], axis=1)
-        vals = jnp.concatenate([
-            jnp.concatenate([kvbuf[ca, 1], kvbuf[cb, 1]], axis=0), jnp.ones((2 * TOK, HW), BF)], axis=1)
+    def more_blocks(si, part, far, *blocks):
+        n = len(blocks) * TOK
+
+        def rows_of(j):
+            got = [kvbuf[c, j] for c in blocks]
+            return got[0] if len(got) == 1 else jnp.concatenate(got, axis=0)
+
+        keys = jnp.concatenate([rows_of(0), kabuf[si, :n]], axis=1)
+        vals = jnp.concatenate([rows_of(1), jnp.ones((n, HW), BF)], axis=1)
+        if far and part == 1:
+            keys, vals = keys[RT:], vals[RT:]
         todo = tiles[part * 4:part * 4 + 4]
         s = scores(*todo[0], keys)
         for i, (h, half) in enumerate(todo):
@@ -293,17 +303,17 @@
         return chip_at(*b), (r1 if b[0] == -1 else r2)
 
     def step(si, part):
-        (ca, va), (cb, vb) = [block(b) for b in STEPS[si]]
-        ca = jnp.where(va, ca, chip)
-        cb = jnp.where(vb, cb, chip)
+        got = [block(b) for b in STEPS[si]]
+        live = got[0][1] if len(got) == 1 else jnp.logical_or(got[0][1], got[1][1])
+        got = [(jnp.where(valid, c, chip), valid) for c, valid in got]
 
         def run():
             if part == 0:
-                put_mask(si, ca, va, 0)
-                put_mask(si, cb, vb, 1)
-            two_blocks(si, ca, cb, part)
-
-        pl.when(jnp.logical_or(va, vb))(run)
+                for n, (c, valid) in enumerate(got):
+                    put_mask(si, c, valid, n)
+            more_blocks(si, part, STEPS[si] == ((-2, 0),), *[c for c, valid in got])
+
+        pl.when(live)(run)
 
     def own_step():
         locals_[2].wait()
@@ -318,8 +328,8 @@
             rows = tile_rows(h, hh)
             abuf[0, core, hh * RT:(hh + 1) * RT, h * HW:(h + 1) * HW] = (
                 acc_ref[rows, :HW] / acc_ref[rows, HW:]).astype(BF)
-        for e, (t, lo, n) in enumerate(CHUNKS):
-            if lo // RT == hh:
+        for e, (t, lo, n, strips) in enumerate(CHUNKS):
+            if lo // RT == hh and strips != 1:
                 to = a_slot(t, core, lo, n)
                 send(a_slot(0, core, lo, n), to, a_recv.at[e, 0],
                      (pair_chip * 2 + core, y) if t == 1 else partner)
@@ -327,61 +337,74 @@
     def way(e):
         return 1 if e % 2 == 0 else -1
 
+    def part_of(e):
+        t, lo, n, strips = CHUNKS[e]
+        return pl.ds(0, n), pl.ds(0, 256 if strips == 2 else HW)
+
     def near(e, up):
-        n = CHUNKS[e][2]
+        at = part_of(e)
         slot = 0 if up == 1 else 1
-        return (near_out.at[e, slot, :n], near_in.at[e, slot, :n], near_recv.at[e, slot])
+        return (near_out.at[(e, slot) + at], near_in.at[(e, slot) + at], near_recv.at[e, slot])
 
     def project(e):
-        t, lo, n = CHUNKS[e]
+        t, lo, n, strips = CHUNKS[e]
+        at = (e,) + part_of(e)
         lhs = jnp.concatenate([abuf[t, 0, lo:lo + n], abuf[t, 1, lo:lo + n]], axis=1)
 
         def part(k):
             q = mod4(y + k)
-            return jnp.dot(lhs, jnp.concatenate([wbuf[0, q], wbuf[1, q]], axis=1), preferred_element_type=F32)
+            rhs = jnp.concatenate([wbuf[0, q], wbuf[1, q]], axis=1) if strips == 2 else wbuf[strips, q]
+            return jnp.dot(lhs, rhs, preferred_element_type=F32)
 
         step = way(e)
-        far_out[e, :n] = part(2).astype(BF)
-        send(far_out.at[e, :n], far_in.at[e, :n], far_recv.at[e], y_at(step))
+        far_out[at] = part(2).astype(BF)
+        send(far_out.at[at], far_in.at[at], far_recv.at[e], y_at(step))
         src, dst, sem = near(e, -step)
         src[...] = part(-step).astype(BF)
         send(src, dst, sem, y_at(-step))
-        hold[e, :n] = part(step)
-        own[e, :n] = part(0)
+        hold[at] = part(step)
+        own[at] = part(0)
 
     def forward(e):
-        n = CHUNKS[e][2]
+        at = (e,) + part_of(e)
         step = way(e)
-        wait(far_in.at[e, :n], far_recv.at[e])
+        wait(far_in.at[at], far_recv.at[e])
         src, dst, sem = near(e, step)
-        src[...] = (hold[e, :n] + far_in[e, :n].astype(F32)).astype(BF)
+        src[...] = (hold[at] + far_in[at].astype(F32)).astype(BF)
         send(src, dst, sem, y_at(step))
 
     out_cols = [pl.ds(pl.multiple_of((2 * zz + core) * HW, HW), HW) for zz in (z, 3 - z)]
 
+    def strips_of(e):
+        strips = CHUNKS[e][3]
+        return ((0, 0), (1, HW)) if strips == 2 else ((strips, 0),)
+
     def finish(e):
-        t, lo, n = CHUNKS[e]
+        t, lo, n, strips = CHUNKS[e]
         hh = lo // RT
+        at = (e,) + part_of(e)
+        total = own[at]
         for up in (1, -1):
             _, dst, sem = near(e, up)
             wait(dst, sem)
-        fin[e, :n] = (own[e, :n] + near_in[e, 0, :n].astype(F32) + near_in[e, 1, :n].astype(F32)).astype(BF)
-        for s in (0, 1):
-            src = fin.at[e, :n, pl.ds(s * HW, HW)]
+            total += dst[...].astype(F32)
+        fin[at] = total.astype(BF)
+        for s, lane in strips_of(e):
+            src = fin.at[e, :n, pl.ds(lane, HW)]
             dst = out_hbm.at[pl.ds(lo - hh * RT, n), out_cols[s]]
             if t == 1:
                 send(src, dst, fin_recv.at[e, core, s], (pair_chip * 2 + hh, y))
             else:
-                pl.when(core == hh)(lambda: pltpu.make_async_copy(src, dst, fin_local.at[s]).start())
+                pl.when(core == hh)(lambda: pltpu.make_async_copy(src, dst, fin_local.at[e, s]).start())
                 send(src, dst, fin_recv.at[e, 0, s], partner, core != hh)
 
     def from_pair(e):
-        _, lo, n = CHUNKS[e]
+        _, lo, n, strips = CHUNKS[e]
         wait(a_slot(1, core, lo, n), a_recv.at[e, 0])
         send(a_slot(1, core, lo, n), a_slot(1, core, lo, n), a_recv.at[e, 1], partner)
 
     def have(e):
-        t, lo, n = CHUNKS[e]
+        t, lo, n, strips = CHUNKS[e]
         wait(a_slot(t, 1 - core, lo, n), a_recv.at[e, t])
 
     actions = {
@@ -405,16 +428,17 @@
             locals_[3].wait()
         actions[name](*args)
 
-    for s in (0, 1):
-        for e, (t, lo, n) in enumerate(CHUNKS):
-            hh = lo // RT
+    for e, (t, lo, n, strips) in enumerate(CHUNKS):
+        hh = lo // RT
+        for s, lane in strips_of(e):
             dst = out_hbm.at[pl.ds(lo - hh * RT, n), out_cols[s]]
             if t == 1:
                 for c in (0, 1):
                     wait(dst, fin_recv.at[e, c, s], core == hh)
             else:
                 wait(dst, fin_recv.at[e, 0, s], core == hh)
-        pltpu.make_async_copy(fin.at[0, :, pl.ds(s * HW, HW)], out_hbm.at[:, out_cols[s]], fin_local.at[s]).wait()
+                pl.when(core == hh)(lambda: pltpu.make_async_copy(
+                    fin.at[e, :n, pl.ds(lane, HW)], dst, fin_local.at[e, s]).wait())
     for c in pair:
         c.wait_send()
     for pred, make in sends:
@@ -431,7 +455,7 @@
         scratch_shapes=[
             pltpu.VMEM((TOK, 512), BF),
             pltpu.VMEM((16, 2, TOK, HW), BF),
-            pltpu.VMEM((4, 2 * TOK, HW), BF),
+            pltpu.VMEM((len(STEPS), 2 * TOK, HW), BF),
             pltpu.VMEM((2, 4, 1024, HW), BF),
             pltpu.VMEM((2048, HW), F32),
             pltpu.VMEM((2048, 2 * HW), F32),
@@ -448,11 +472,11 @@
             pltpu.SemaphoreType.DMA((3,)),
             pltpu.SemaphoreType.DMA((4, 16)),
             pltpu.SemaphoreType.DMA((4, 4)),
-            pltpu.SemaphoreType.DMA((160,)),
+            pltpu.SemaphoreType.DMA((192,)),
             pltpu.SemaphoreType.DMA((N, 2)),
             pltpu.SemaphoreType.DMA((N,)),
             pltpu.SemaphoreType.DMA((N, 2)),
-            pltpu.SemaphoreType.DMA((2,)),
+            pltpu.SemaphoreType.DMA((N, 2)),
             pltpu.SemaphoreType.DMA((N, 2, 2)),
         ],
         compiler_params=pltpu.CompilerParams(

time: 67.8 us -> 66.7 us (0.984)
  no operation moved by 1% of the time
where the time goes in v4:
time: 66.7 us; the launch traced here: 66.4 us
  Pallas kernels  64.6 us (97%)
  local copies, waits for them, and re-layouts  1.87 us (3%)
    pallas_call x1, Pallas kernels, shards(): pl.pallas_call(kernel, out_shape=jax.ShapeDtypeStruct((256, 1024), BF), i...  64.6 us
    unnamed x1, local copies, waits for them, and re-layouts  1.87 us

profile of v4, /device:TPU:5, one launch (start us, length us, event | category | flops | bytes accessed | tf_op | source)
XLA Modules:
  0.0 66.4 jit_solution(7760559921966102698)
XLA Ops:
  0.0 64.6 %attention_projection.1 = bf16[256,1024]{1,0:T(8,128)(2,1)} custom-call(bf16[256,1024]{1,0:T(8,128)(2,1)} %q_hbm.1, bf16[256,256]{1,0:T(8,128)(2,1)} %k_hbm.1, bf16[256,256]{1,0:T(8,128)(2,1)} %v_hbm.1, s32[64,128]{1,0:T(8,128)} %bitcast.1, bf16[1024,128]{1,0:T(8,128)(2,1)} %w_hbm.1), custom_call_target="tpu_custom_call" | custom-call | tf_op jit(solution)/shard_map/attention_projection/pallas_call | solution.py:450
  64.6 1.9 %copy.7 = bf16[256,1024]{1,0:T(8,128)(2,1)} copy(bf16[256,1024]{1,0:T(8,128)(2,1)} %attention_projection.1) | data formatting | bytes 1048576

commit v5 on v4

--- a/solution.py
+++ b/solution.py
@@ -19,28 +19,25 @@
 N = len(CHUNKS)
 STEPS = (
     ((-1, 0),),
+    ((-2, 0),),
     ((-1, -1), (-1, 1)),
-    ((-2, 0),),
-    ((-1, 2),),
-    ((0, -1),),
-    ((0, 1),),
-    ((0, 2),),
+    ((-1, 2), (0, -1)),
+    ((0, 1), (0, 2)),
 )
 ORDER = (
-    ("cr", 0), ("cr", 1), ("ko", 0, 0), ("ko", 0, 1), ("ko", 1, 1), ("ko", 1, 0), ("wo", 1, -1), ("X1", 0, 0),
-    ("X1", 1, 0), ("wo", 0, 1), ("B", 0), ("B", 1), ("X1", 1, 1), ("wc", 0), ("own",), ("X2", 0, 0), ("X1", 0, 1),
-    ("wc", 1), ("X2", 1, 1), ("wo", 0, -1), ("X2", 1, 0), ("X2", 0, 1), ("wr", 0, 0), ("c", 0, 0), ("L1", 1, 1),
-    ("R2", 0, 0), ("wo", 1, 1), ("Ra", 0, 0), ("c", 2, 0), ("L1", 0, 1), ("R0", 0, 0), ("c", 0, 1), ("Ra", 1, 0),
-    ("R2", 1, 1), ("R0", 1, 1), ("L1", 0, 0), ("wr", 0, 1), ("c", 2, 1), ("R2", 1, 0), ("Rb", 0, 0), ("R0", 0, 1),
-    ("wr", 1, 0), ("ww", 1, 0), ("R0", 1, 0), ("wr", 1, 1), ("Ra", 1, 1), ("L1", 1, 0), ("L3", 1, 1), ("L3", 0, 0),
-    ("L3", 1, 0), ("R2", 0, 1), ("c", 5, 0), ("L3", 0, 1), ("Ra", 0, 1), ("Rb", 1, 0), ("Rb", 1, 1), ("Rb", 0, 1),
-    ("c", 1, 0), ("ww", 1, 1), ("c", 4, 0), ("L0", 0, 0), ("L2", 0, 0), ("c", 1, 1), ("E", 0, 0), ("E", 0, 1),
-    ("L0", 1, 0), ("L0", 0, 1), ("E", 1, 0), ("E", 1, 1), ("L2", 1, 0), ("L0", 1, 1), ("c", 6, 0), ("L2", 1, 1),
-    ("L2", 0, 1), ("c", 3, 0), ("at", 0), ("ww", 0, 1), ("c", 4, 1), ("c", 6, 1), ("wf", 0, 0), ("wf", 1, 0),
-    ("wf", 0, 1), ("wf", 1, 1), ("h", 0), ("c", 5, 1), ("ww", 0, 0), ("p", 0), ("c", 3, 1), ("g", 2), ("at", 1),
-    ("h", 2), ("p", 2), ("g", 3), ("h", 1), ("p", 1), ("h", 3), ("g", 4), ("p", 3), ("f", 2), ("h", 4), ("p", 4),
-    ("g", 5), ("h", 5), ("p", 5), ("f", 3), ("x", 2), ("f", 4), ("f", 5), ("f", 1), ("f", 0), ("x", 3), ("x", 4),
-    ("x", 5), ("x", 0), ("x", 1),
+    ("cr", 0), ("cr", 1), ("ko", 0, 0), ("ko", 0, 1), ("ko", 1, 1), ("ko", 1, 0), ("own",), ("B", 1), ("X1", 0, 0),
+    ("X1", 1, 0), ("wo", 0, 1), ("wc", 0), ("X2", 1, 1), ("B", 0), ("wo", 1, 1), ("wc", 1), ("X2", 0, 0),
+    ("X1", 0, 1), ("ww", 1, 0), ("wo", 1, -1), ("X2", 1, 0), ("X2", 0, 1), ("X1", 1, 1), ("c", 0, 0), ("c", 0, 1),
+    ("R2", 0, 0), ("c", 1, 0), ("R0", 0, 0), ("wr", 0, 0), ("R0", 0, 1), ("Ra", 1, 0), ("wr", 1, 0), ("wo", 0, -1),
+    ("R2", 0, 1), ("R2", 1, 0), ("Ra", 0, 1), ("L1", 1, 1), ("wr", 1, 1), ("Rb", 0, 0), ("Ra", 0, 0), ("R0", 1, 0),
+    ("c", 1, 1), ("Rb", 1, 0), ("L3", 0, 1), ("Ra", 1, 1), ("L3", 1, 1), ("Rb", 0, 1), ("Rb", 1, 1), ("R0", 1, 1),
+    ("L1", 1, 0), ("wr", 0, 1), ("R2", 1, 1), ("L1", 0, 1), ("c", 2, 0), ("ww", 0, 1), ("L3", 0, 0), ("L1", 0, 0),
+    ("c", 2, 1), ("L2", 1, 1), ("L2", 1, 0), ("L2", 0, 1), ("L3", 1, 0), ("E", 0, 1), ("E", 1, 1), ("L2", 0, 0),
+    ("L0", 0, 0), ("c", 3, 0), ("E", 0, 0), ("E", 1, 0), ("ww", 1, 1), ("L0", 0, 1), ("L0", 1, 0), ("L0", 1, 1),
+    ("c", 4, 0), ("at", 0), ("ww", 0, 0), ("c", 3, 1), ("wf", 0, 0), ("c", 4, 1), ("wf", 0, 1), ("h", 0),
+    ("wf", 1, 1), ("wf", 1, 0), ("p", 0), ("g", 2), ("at", 1), ("h", 2), ("p", 2), ("g", 3), ("h", 1), ("p", 1),
+    ("f", 2), ("g", 4), ("h", 3), ("p", 3), ("h", 4), ("p", 4), ("g", 5), ("h", 5), ("p", 5), ("f", 3), ("f", 4),
+    ("x", 2), ("f", 0), ("f", 5), ("x", 3), ("f", 1), ("x", 4), ("x", 5), ("x", 0), ("x", 1),
 )
 
 def kernel(q_hbm, k_hbm, v_hbm, seg_ref, w_hbm, out_hbm,

time: 66.7 us -> 66.5 us (level)
  no operation moved by 1% of the time
where the time goes in v5:
time: 66.5 us; the launch traced here: 66.3 us
  Pallas kernels  64.4 us (97%)
  local copies, waits for them, and re-layouts  1.87 us (3%)
    pallas_call x1, Pallas kernels, shards(): pl.pallas_call(kernel, out_shape=jax.ShapeDtypeStruct((256, 1024), BF), i...  64.4 us
    unnamed x1, local copies, waits for them, and re-layouts  1.87 us

profile of v5, /device:TPU:5, one launch (start us, length us, event | category | flops | bytes accessed | tf_op | source)
XLA Modules:
  0.0 66.3 jit_solution(5366487080320951593)
XLA Ops:
  0.0 64.4 %attention_projection.1 = bf16[256,1024]{1,0:T(8,128)(2,1)} custom-call(bf16[256,1024]{1,0:T(8,128)(2,1)} %q_hbm.1, bf16[256,256]{1,0:T(8,128)(2,1)} %k_hbm.1, bf16[256,256]{1,0:T(8,128)(2,1)} %v_hbm.1, s32[64,128]{1,0:T(8,128)} %bitcast.1, bf16[1024,128]{1,0:T(8,128)(2,1)} %w_hbm.1), custom_call_target="tpu_custom_call" | custom-call | tf_op jit(solution)/shard_map/attention_projection/pallas_call | solution.py:447
  64.4 1.9 %copy.7 = bf16[256,1024]{1,0:T(8,128)(2,1)} copy(bf16[256,1024]{1,0:T(8,128)(2,1)} %attention_projection.1) | data formatting | bytes 1048576

commit v6 on v5

--- a/solution.py
+++ b/solution.py
@@ -176,12 +176,11 @@
         hot = (lax.broadcasted_iota(jnp.int32, (HW, TOK), 0) == row).astype(F32)
         return hot.T
 
-    own_hot = onehot(chip)
-    qa = (own_hot * (-BIG)).astype(BF)
+    masks = {}
 
     def scores(h, half, keys):
         qq = qbuf[half * RT:(half + 1) * RT, h * HW:(h + 1) * HW]
-        qc = jnp.concatenate([qq, qa[half * RT:(half + 1) * RT]], axis=1)
+        qc = jnp.concatenate([qq, masks["q"][half * RT:(half + 1) * RT]], axis=1)
         return lax.dot_general(qc, keys, (((1,), (1,)), ((), ())), preferred_element_type=F32)
 
     def weights(s, mp):
@@ -196,6 +195,8 @@
         return slice((h * 2 + half) * RT, (h * 2 + half + 1) * RT)
 
     def own_block():
+        own_hot = onehot(chip)
+        masks["q"] = (own_hot * (-BIG)).astype(BF)
         keys = jnp.concatenate([kvbuf[chip, 0], (1.0 - own_hot).astype(BF)], axis=1)
         vals = jnp.concatenate([kvbuf[chip, 1], jnp.ones((TOK, HW), BF)], axis=1)
 

time: 66.5 us -> 66.5 us (level)
  no operation moved by 1% of the time
where the time goes in v6:
time: 66.5 us; the launch traced here: 66.2 us
  Pallas kernels  64.4 us (97%)
  local copies, waits for them, and re-layouts  1.87 us (3%)
    pallas_call x1, Pallas kernels, shards(): pl.pallas_call(kernel, out_shape=jax.ShapeDtypeStruct((256, 1024), BF), i...  64.4 us
    unnamed x1, local copies, waits for them, and re-layouts  1.87 us

profile of v6, /device:TPU:5, one launch (start us, length us, event | category | flops | bytes accessed | tf_op | source)
XLA Modules:
  0.0 66.2 jit_solution(4762553934057160144)
XLA Ops:
  0.0 64.4 %attention_projection.1 = bf16[256,1024]{1,0:T(8,128)(2,1)} custom-call(bf16[256,1024]{1,0:T(8,128)(2,1)} %q_hbm.1, bf16[256,256]{1,0:T(8,128)(2,1)} %k_hbm.1, bf16[256,256]{1,0:T(8,128)(2,1)} %v_hbm.1, s32[64,128]{1,0:T(8,128)} %bitcast.1, bf16[1024,128]{1,0:T(8,128)(2,1)} %w_hbm.1), custom_call_target="tpu_custom_call" | custom-call | tf_op jit(solution)/shard_map/attention_projection/pallas_call | solution.py:448
  64.4 1.9 %copy.7 = bf16[256,1024]{1,0:T(8,128)(2,1)} copy(bf16[256,1024]{1,0:T(8,128)(2,1)} %attention_projection.1) | data formatting | bytes 1048576

commit v7 on v6

--- a/solution.py
+++ b/solution.py
@@ -18,26 +18,25 @@
 CHUNKS = ((0, 0, 256, 2), (0, 256, 256, 2), (1, 0, 128, 2), (1, 128, 128, 2), (1, 256, 128, 2), (1, 384, 128, 2))
 N = len(CHUNKS)
 STEPS = (
-    ((-1, 0),),
-    ((-2, 0),),
+    ((-1, 0), (-2, 0)),
     ((-1, -1), (-1, 1)),
     ((-1, 2), (0, -1)),
     ((0, 1), (0, 2)),
 )
 ORDER = (
-    ("cr", 0), ("cr", 1), ("ko", 0, 0), ("ko", 0, 1), ("ko", 1, 1), ("ko", 1, 0), ("own",), ("B", 1), ("X1", 0, 0),
-    ("X1", 1, 0), ("wo", 0, 1), ("wc", 0), ("X2", 1, 1), ("B", 0), ("wo", 1, 1), ("wc", 1), ("X2", 0, 0),
-    ("X1", 0, 1), ("ww", 1, 0), ("wo", 1, -1), ("X2", 1, 0), ("X2", 0, 1), ("X1", 1, 1), ("c", 0, 0), ("c", 0, 1),
-    ("R2", 0, 0), ("c", 1, 0), ("R0", 0, 0), ("wr", 0, 0), ("R0", 0, 1), ("Ra", 1, 0), ("wr", 1, 0), ("wo", 0, -1),
-    ("R2", 0, 1), ("R2", 1, 0), ("Ra", 0, 1), ("L1", 1, 1), ("wr", 1, 1), ("Rb", 0, 0), ("Ra", 0, 0), ("R0", 1, 0),
-    ("c", 1, 1), ("Rb", 1, 0), ("L3", 0, 1), ("Ra", 1, 1), ("L3", 1, 1), ("Rb", 0, 1), ("Rb", 1, 1), ("R0", 1, 1),
-    ("L1", 1, 0), ("wr", 0, 1), ("R2", 1, 1), ("L1", 0, 1), ("c", 2, 0), ("ww", 0, 1), ("L3", 0, 0), ("L1", 0, 0),
-    ("c", 2, 1), ("L2", 1, 1), ("L2", 1, 0), ("L2", 0, 1), ("L3", 1, 0), ("E", 0, 1), ("E", 1, 1), ("L2", 0, 0),
-    ("L0", 0, 0), ("c", 3, 0), ("E", 0, 0), ("E", 1, 0), ("ww", 1, 1), ("L0", 0, 1), ("L0", 1, 0), ("L0", 1, 1),
-    ("c", 4, 0), ("at", 0), ("ww", 0, 0), ("c", 3, 1), ("wf", 0, 0), ("c", 4, 1), ("wf", 0, 1), ("h", 0),
-    ("wf", 1, 1), ("wf", 1, 0), ("p", 0), ("g", 2), ("at", 1), ("h", 2), ("p", 2), ("g", 3), ("h", 1), ("p", 1),
-    ("f", 2), ("g", 4), ("h", 3), ("p", 3), ("h", 4), ("p", 4), ("g", 5), ("h", 5), ("p", 5), ("f", 3), ("f", 4),
-    ("x", 2), ("f", 0), ("f", 5), ("x", 3), ("f", 1), ("x", 4), ("x", 5), ("x", 0), ("x", 1),
+    ("cr", 0), ("cr", 1), ("ko", 0, 0), ("ko", 1, 0), ("ko", 0, 1), ("ko", 1, 1), ("wo", 1, -1), ("X1", 0, 0),
+    ("B", 1), ("B", 0), ("X1", 1, 0), ("wc", 0), ("X1", 0, 1), ("X2", 0, 0), ("wo", 0, 1), ("X2", 1, 0), ("own",),
+    ("X2", 0, 1), ("X1", 1, 1), ("wc", 1), ("X2", 1, 1), ("R0", 0, 0), ("R0", 1, 0), ("wr", 1, 0), ("Ra", 0, 0),
+    ("wo", 0, -1), ("c", 0, 0), ("R2", 1, 0), ("wr", 0, 1), ("R0", 0, 1), ("R2", 0, 1), ("L1", 0, 1), ("L1", 0, 0),
+    ("Ra", 0, 1), ("wo", 1, 1), ("Ra", 1, 0), ("Rb", 0, 0), ("c", 0, 1), ("R2", 1, 1), ("Ra", 1, 1), ("R2", 0, 0),
+    ("R0", 1, 1), ("Rb", 0, 1), ("Rb", 1, 0), ("Rb", 1, 1), ("L3", 0, 0), ("wr", 0, 0), ("c", 1, 0), ("L3", 1, 1),
+    ("wr", 1, 1), ("E", 0, 1), ("E", 1, 0), ("c", 1, 1), ("L0", 0, 1), ("L2", 0, 0), ("E", 0, 0), ("L3", 0, 1),
+    ("L2", 0, 1), ("L2", 1, 1), ("L1", 1, 0), ("L3", 1, 0), ("L2", 1, 0), ("E", 1, 1), ("c", 2, 0), ("L1", 1, 1),
+    ("L0", 0, 0), ("L0", 1, 1), ("L0", 1, 0), ("c", 3, 0), ("at", 0), ("c", 3, 1), ("ww", 1, 0), ("ww", 0, 0),
+    ("ww", 0, 1), ("ww", 1, 1), ("h", 0), ("c", 2, 1), ("wf", 1, 1), ("wf", 0, 0), ("wf", 0, 1), ("wf", 1, 0),
+    ("p", 0), ("g", 2), ("at", 1), ("h", 2), ("p", 2), ("h", 1), ("g", 3), ("p", 1), ("h", 3), ("g", 4), ("p", 3),
+    ("f", 2), ("h", 4), ("p", 4), ("g", 5), ("h", 5), ("p", 5), ("f", 3), ("f", 4), ("x", 2), ("f", 5), ("f", 0),
+    ("f", 1), ("x", 3), ("x", 4), ("x", 5), ("x", 0), ("x", 1),
 )
 
 def kernel(q_hbm, k_hbm, v_hbm, seg_ref, w_hbm, out_hbm,

time: 66.5 us -> 65.9 us (level)
  Pallas kernels: 64.4 us -> 63.4 us
    pallas_call x1, Pallas kernels: 64.4 us -> 63.4 us  [shards(): pl.pallas_call(kernel, out_shape=jax.ShapeDtypeStruct((256, 1024), BF), i...]
where the time goes in v7:
time: 65.9 us; the launch traced here: 65.3 us
  Pallas kernels  63.4 us (96%)
  local copies, waits for them, and re-layouts  1.87 us (3%)
    pallas_call x1, Pallas kernels, shards(): pl.pallas_call(kernel, out_shape=jax.ShapeDtypeStruct((256, 1024), BF), i...  63.4 us
    unnamed x1, local copies, waits for them, and re-layouts  1.87 us

profile of v7, /device:TPU:5, one launch (start us, length us, event | category | flops | bytes accessed | tf_op | source)
XLA Modules:
  0.0 65.3 jit_solution(5314908323398065933)
XLA Ops:
  0.0 63.4 %attention_projection.1 = bf16[256,1024]{1,0:T(8,128)(2,1)} custom-call(bf16[256,1024]{1,0:T(8,128)(2,1)} %q_hbm.1, bf16[256,256]{1,0:T(8,128)(2,1)} %k_hbm.1, bf16[256,256]{1,0:T(8,128)(2,1)} %v_hbm.1, s32[64,128]{1,0:T(8,128)} %bitcast.1, bf16[1024,128]{1,0:T(8,128)(2,1)} %w_hbm.1), custom_call_target="tpu_custom_call" | custom-call | tf_op jit(solution)/shard_map/attention_projection/pallas_call | solution.py:447
  63.4 1.9 %copy.7 = bf16[256,1024]{1,0:T(8,128)(2,1)} copy(bf16[256,1024]{1,0:T(8,128)(2,1)} %attention_projection.1) | data formatting | bytes 1048576
